TPU v7x, 32 devices: a whole 2x2x4 slice. The times are simulated.
32 devices in a mesh: groups: 1, kcol: 16 (over z, y, x), qrow: 2 (over core).
Axes of the slice: x: 2, y: 2, z: 4, core: 2. Of those that a mesh axis runs over, the one named last changes fastest.
Arguments:
- queries: bfloat16 [128, 1024], P(('groups', 'kcol', 'qrow')), may hold values from -120 to 120
- key_value: bfloat16 [24576, 256], P(('groups', 'kcol')), may hold values from -6 to 6
- block_lists: int32 [1, 64], P('groups'), may hold values from 0 to 191, as said below
Outputs:
- attended: bfloat16 [128, 1024], P(('groups', 'kcol', 'qrow'))
Inputs may be any that keep to these rules, and one draw needn't show every extreme that they name: `block_lists`: row i names 64 distinct key blocks, none after block 191 + i (the block that holds query block i); it always names that block, the 11 blocks just before it, and block 0.
All inputs are finite; a program needn't handle non-finite values.
Results may differ from a plain program's by a relative error of at most 0.0065.
Values may be sent and summed in bfloat16 or wider, within the bound.
No kernel may reach another device: no remote copies, remote signals or barrier semaphores. Data moves between devices by JAX's collectives and lax.ppermute only.
A program may use at most 128 MiB of HBM per device.

v0:
```python
import math

import jax
import jax.numpy as jnp
from jax import lax
from jax.sharding import PartitionSpec as P

BLK = 128


masked_score = -1e30


def combined_all(part, axis, combine):
    gathered = jax.tree.map(lambda a: lax.all_gather(a, axis), part)

    def take(source):
        return jax.tree.map(lambda a: lax.dynamic_index_in_dim(a, source, 0, False), gathered)

    return lax.fori_loop(
        1, lax.axis_size(axis), lambda source, state: combine(state, take(source)), take(0)
    )


def partial_softmax(query_tile, key_rows, value_rows, visible):
    score_scale = 1.0 / math.sqrt(key_rows.shape[1])
    scores = (
        jnp.einsum("thd,kd->htk", query_tile, key_rows, preferred_element_type=jnp.float32)
        * score_scale
    )
    scores = jnp.where(visible[None], scores, masked_score)
    row_max = jnp.max(scores, axis=-1)
    weights = jnp.where(visible[None], jnp.exp(scores - row_max[..., None]), 0.0)
    row_total = jnp.sum(weights, axis=-1)
    numerator = jnp.einsum(
        "htk,kd->thd", weights.astype(jnp.bfloat16), value_rows, preferred_element_type=jnp.float32
    )
    return (jnp.transpose(row_max), jnp.transpose(row_total), numerator)


def combine_partials(left_part, right_part):
    max_left, total_left, numer_left = left_part
    max_right, total_right, numer_right = right_part
    row_max = jnp.maximum(max_left, max_right)
    scale_left = jnp.exp(max_left - row_max)
    scale_right = jnp.exp(max_right - row_max)
    return (
        row_max,
        total_left * scale_left + total_right * scale_right,
        numer_left * scale_left[..., None] + numer_right * scale_right[..., None],
    )


def per_device(queries, key_value, block_lists):
    column_count = lax.axis_size("kcol")
    column = lax.axis_index("kcol")
    row_count = lax.axis_size("qrow")
    row_index = lax.axis_index("qrow")
    tok_dev = queries.shape[0]
    feature_count = queries.shape[1]
    head_dim = key_value.shape[1] // 2
    head_count = feature_count // head_dim
    stored = key_value.shape[0] // BLK
    all_blocks = stored * column_count
    gathered = lax.all_gather(queries, "kcol", axis=0, tiled=True)
    gathered_rows = gathered.shape[0]
    tile_rows = BLK // row_count
    query_blocks = gathered_rows // tile_rows
    offset = (all_blocks - query_blocks) * BLK
    gather_pos = jnp.arange(gathered_rows, dtype=jnp.int32)
    token_index = (gather_pos // tok_dev * row_count + row_index) * tok_dev + gather_pos % tok_dev
    query_pos = (offset + token_index).reshape(query_blocks, tile_rows)
    query_tiles = gathered.reshape(query_blocks, tile_rows, head_count, head_dim)
    block_ids = column * stored + jnp.arange(stored, dtype=jnp.int32)
    key_pos = column * stored * BLK + jnp.arange(stored * BLK, dtype=jnp.int32)
    key_rows = key_value[:, :head_dim]
    value_rows = key_value[:, head_dim:]

    def one_block(inputs):
        query_tile, positions, listed = inputs
        listed_here = jnp.any(listed[:, None] == block_ids[None, :], axis=0)
        usable = jnp.repeat(listed_here, BLK, total_repeat_length=stored * BLK)
        visible = usable[None, :] & (key_pos[None, :] <= positions[:, None])
        return partial_softmax(query_tile, key_rows, value_rows, visible)

    row_max, row_total, numerator = lax.map(one_block, (query_tiles, query_pos, block_lists))
    row_max = row_max.reshape(gathered_rows, head_count)
    row_total = row_total.reshape(gathered_rows, head_count)
    numerator = numerator.reshape(gathered_rows, head_count, head_dim)
    merged = combined_all((row_max, row_total, numerator), "kcol", combine_partials)
    first_row = column * tok_dev
    summed_total = lax.dynamic_slice_in_dim(merged[1], first_row, tok_dev, 0)
    summed_numer = lax.dynamic_slice_in_dim(merged[2], first_row, tok_dev, 0)
    attended = summed_numer / summed_total[..., None]
    return attended.reshape(tok_dev, feature_count).astype(jnp.bfloat16)


def solution(mesh):
    placed = (P(("groups", "kcol", "qrow"), None), P(("groups", "kcol"), None), P("groups", None))
    return jax.shard_map(
        per_device,
        mesh=mesh,
        in_specs=placed,
        out_specs=P(("groups", "kcol", "qrow"), None),
        check_vma=False,
    )
```

profile of v0, /device:TPU:0, one launch (start us, length us, event | category | flops | bytes accessed | tf_op | source)
XLA Modules:
  0.0 169.5 jit_solution(10916630586948243898)
XLA Ops:
  6.6 0.8 compare_reduce_fusion.5
  7.4 0.7 fusion.37
  8.1 43.3 %all-gather.3 = bf16[16,4,1024]{2,1,0:T(4,128)(2,1)S(1)} all-gather(bf16[1,4,1024]{2,1,0:T(4,128)(2,1)} %bitcast.104), channel_id=1, replica_groups=mesh['groups'=1,'kcol'=16,'qrow'=2] {'kcol'}, dimensions={0}, use_global_device_ids=true | all-gather | bytes 139264 | tf_op jit(solution)/shard_map/all_gather | solution.py:65
  51.5 4.5 %select_reduce_fusion = (pred[1536]{0:T(1024)(128)(4,1)S(1)}, pred[1536]{0:T(1024)(128)(4,1)S(1)}, pred[1536]{0:T(1024)(128)(4,1)S(1)}, pred[1536]{0:T(1024)(128...) fusion(pred[]{:T(512)} %bitcast.11, pred[]{:T(512)} %bitcast.12, pred[]{:T(512)} %bitcast.13, ...), kind=kLoop, calls=%fused_computation.28 | loop fusion | flops 29184 | bytes 21511 | tf_op jit(solution)/shard_map/while/body/eval_jaxpr/jit(_take)/gather | solution.py:82
  56.0 3.2 %fusion.29 = pred[1536]{0:T(1024)(128)(4,1)S(1)} fusion(pred[1536]{0:T(1024)(128)(4,1)S(1)} %get-tuple-element.267, pred[1536]{0:T(1024)(128)(4,1)S(1)} %get-tuple-element.266, pred[1536]{0:T(1024)(128)(4,1)S(1)} %get-tuple-element.265, pred[1536]{0:T(1024)(128)(4,1)S(1)} %get-tuple-element.263, pred[1536]{0:T(1024)(128)(4,1)S(1)} %get-tuple-element.264, ...), kind=kLoop, calls=%fused_computation.47 | loop fusion | flops 21504 | bytes 10757 | tf_op jit(solution)/shard_map/while/body/eval_jaxpr/jit(_take)/select_n | solution.py:82
  59.2 0.1 compare_and_fusion
  59.4 1.7 %fusion.38 = (f32[8,64]{1,0:T(8,128)S(1)}, f32[8,64,1536]{2,1,0:T(8,128)S(1)}) fusion(bf16[64,8,128]{2,1,0:T(8,128)(2,1)S(1)} %squeeze.51, bf16[1536,256]{1,0:T(8,128)(2,1)} %param.8, pred[64,1536]{1,0:T(8,128)(4,1)S(1)} %compare_and_fusion), kind=kOutput, calls=%fused_computation.65 | convolution fusion | flops 203685376 | bytes 3770368 | tf_op jit(solution)/shard_map/while/body/eval_jaxpr/thd,kd->htk/dot_general | solution.py:28
  61.1 1.3 fusion.13
  62.5 0.7 fusion.7
  63.2 36.2 %all-gather.5 = f32[16,64,8]{1,2,0:T(8,128)S(1)} all-gather(f32[1,64,8]{1,2,0:T(8,128)S(1)} %bitcast.103), channel_id=3, replica_groups=mesh['groups'=1,'kcol'=16,'qrow'=2] {'kcol'}, dimensions={0}, use_global_device_ids=true | all-gather | bytes 34816 | tf_op jit(solution)/shard_map/all_gather | solution.py:15
  99.4 39.0 %all-gather.4 = f32[16,64,8]{1,2,0:T(8,128)S(1)} all-gather(f32[1,64,8]{1,2,0:T(8,128)S(1)} %bitcast.102), channel_id=2, replica_groups=mesh['groups'=1,'kcol'=16,'qrow'=2] {'kcol'}, dimensions={0}, use_global_device_ids=true | all-gather | bytes 34816 | tf_op jit(solution)/shard_map/all_gather | solution.py:15
  138.4 1.0 slice.53
  139.4 0.2 copy.24
  139.6 22.3 %while.26 = (s32[]{:T(128)}, f32[64,8]{0,1:T(8,128)S(1)}, f32[64,8]{0,1:T(8,128)S(1)}, f32[64,8,128]{2,1,0:T(8,128)S(1)}, f32[16,64,8]{1,2,0:T(8,128)S(1)}, /*in...) while((s32[]{:T(128)}, f32[64,8]{0,1:T(8,128)S(1)}, ...), condition=%wide.region_4.5_spmd, body=%wide.region_3.4_spmd.sunk | while | flops 199685 | bytes 1339535 | solution.py:20
  139.6 0.1 copy.48
  139.7 0.1 copy.49
  139.8 1.0 constant_dynamic-slice_fusion.3
  140.7 0.3 fusion.42
  141.1 0.1 copy.48
  141.2 0.1 copy.49
  141.3 1.0 constant_dynamic-slice_fusion.3
  142.2 0.3 fusion.42
  142.6 0.1 copy.48
  142.7 1.0 constant_dynamic-slice_fusion.3
  143.7 0.3 fusion.42
  144.1 0.1 copy.48
  144.2 1.0 constant_dynamic-slice_fusion.3
  145.2 0.3 fusion.42
  145.5 0.1 copy.48
  145.7 1.0 constant_dynamic-slice_fusion.3
  146.7 0.3 fusion.42
  147.0 0.1 copy.48
  147.2 1.0 constant_dynamic-slice_fusion.3
  148.2 0.3 fusion.42
  148.5 0.1 copy.48
  148.7 1.0 constant_dynamic-slice_fusion.3
  149.7 0.3 fusion.42
  150.0 0.1 copy.48
  150.1 0.1 copy.49
  150.2 1.0 constant_dynamic-slice_fusion.3
  151.1 0.3 fusion.42
  151.5 0.1 copy.48
  151.7 1.0 constant_dynamic-slice_fusion.3
  152.6 0.3 fusion.42
  153.0 0.1 copy.48
  153.1 1.0 constant_dynamic-slice_fusion.3
  154.1 0.3 fusion.42
  154.5 0.1 copy.48
  154.6 1.0 constant_dynamic-slice_fusion.3
  155.6 0.3 fusion.42
  155.9 0.1 copy.48
  156.1 1.0 constant_dynamic-slice_fusion.3
  157.1 0.3 fusion.42
  157.4 0.1 copy.48
  157.6 1.0 constant_dynamic-slice_fusion.3
  158.6 0.3 fusion.42
  158.9 0.1 copy.48
  159.1 1.0 constant_dynamic-slice_fusion.3
  160.1 0.3 fusion.42
  160.4 0.1 copy.48
  160.6 1.0 constant_dynamic-slice_fusion.3
  161.5 0.3 fusion.42
  161.9 0.1 copy.26
  162.1 0.6 copy.43
  (41 shorter events, 1.5 us)
Async XLA Ops:
  6.5 131.9 %all-gather.8.cloned.1.call-start = ((), (), s32[]{:S(2)}) async-start(), calls=%async_computation | async-start | bytes 4456448 | tf_op jit(solution)/shard_map/all_gather | solution.py:15
  51.5 9.6 %copy-start = (bf16[1536,256]{1,0:T(8,128)(2,1)S(1)}, bf16[1536,256]{1,0:T(8,128)(2,1)}, u32[]{:S(2)}) copy-start(bf16[1536,256]{1,0:T(8,128)(2,1)} %param.8) | copy-start | bytes 2359300
Sparse Core Ops, SparseCore 0:
  62.6 72.8 all-gather.7
where the time goes:
time: 170 us
  blocking collectives  119 us (70%)
  local copies, waits for them, and re-layouts  19.7 us (12%)
  other arithmetic  14.2 us (8%)
  between operations  13.5 us (8%)
  matrix products  3.06 us (2%)
    all_gather x2, blocking collectives, combined_all(): gathered = jax.tree.map(lambda a: lax.all_gather(a, axis), part)  75.2 us
    all_gather x1, blocking collectives, per_device(): gathered = lax.all_gather(queries, 'kcol', axis=0, tiled=True)  43.3 us
    dynamic_slice x18, local copies, waits for them, and re-layouts, take(): lax.dynamic_index_in_dim(a, source, 0, False)  15.5 us
    gather x1, other arithmetic, one_block(): usable = jnp.repeat(listed_here, BLK, total_repeat_length=stored * BLK)  4.49 us
    add x15, other arithmetic, combine_partials(): numer_left * scale_left[..., None] + numer_right * scale_right[..., None]  4.46 us
  transfers between devices with their start and end apart: 1, of which 0 were waited for; matrix products, arithmetic and copies ran while one was open for 0% of the time, Pallas kernels for 0%

commit v1 on v0

v1 whole, which is shorter than its diff:
```python
import functools
import math

import jax
import jax.numpy as jnp
from jax import lax
from jax.experimental import pallas as pl
from jax.experimental.pallas import tpu as pltpu
from jax.sharding import PartitionSpec as P


BLK = 128
LANES = 128
hidden_score = -1e30
floor_score = -1e29


def swap_pairs(size, mask):
    return [(i, i ^ mask) for i in range(size)]


def attend_kernel(plan, info, *refs):
    tokens, heads, dim, groups, masks, tok_dev, row_count, first_query, spans = plan
    q_parts, kv_parts, (keep, send, scores) = refs[:2], refs[2:-3], refs[-3:]
    rows = heads * tokens
    scale = math.log2(math.e) / math.sqrt(dim)
    blocks = [(part, i) for part, ref in enumerate(kv_parts) for i in range(ref.shape[0] // BLK)]
    count = len(blocks)
    query = jnp.concatenate(
        [
            jnp.concatenate([part[:, h * dim : (h + 1) * dim] for part in q_parts], axis=0)
            for h in range(heads)
        ],
        axis=0,
    )
    column, row_index = info[(groups + 1) * count], info[(groups + 1) * count + 1]
    t = lax.rem(lax.broadcasted_iota(jnp.int32, (rows, BLK), 0), tokens)
    source = lax.div(t, tok_dev)
    relative = jnp.zeros_like(t)
    for k, mask in enumerate(masks):
        relative += ((source >> k) & 1) * mask
    token = ((relative ^ column) * row_count + row_index) * tok_dev + lax.rem(t, tok_dev)
    lane = lax.broadcasted_iota(jnp.int32, (rows, BLK), 1)

    def bias_of(b):
        out = jnp.where(info[b] > 0, 0.0, hidden_score).astype(jnp.float32)
        for g in range(1, groups):
            other = jnp.where(info[g * count + b] > 0, 0.0, hidden_score).astype(jnp.float32)
            out = jnp.where(lax.div(token, BLK) == g, other, out)
        return out

    top = jnp.full((rows, BLK), floor_score, jnp.float32)
    for b, (part, i) in enumerate(blocks):
        keys = kv_parts[part][i * BLK : (i + 1) * BLK, :dim]
        s = lax.dot_general(
            query, keys, (((1,), (1,)), ((), ())), preferred_element_type=jnp.float32
        )
        s = s + bias_of(b)
        if i >= spans[part]:
            key_pos = info[groups * count + b] * BLK + lane
            s = jnp.where(key_pos <= first_query + token, s, hidden_score)
        scores[:, b * BLK : (b + 1) * BLK] = s
        top = jnp.maximum(top, s)
    row_max = jnp.max(top, axis=1, keepdims=True)
    total = jnp.zeros((rows, BLK), jnp.float32)
    numer = jnp.zeros((rows, dim), jnp.float32)
    base = 0
    for ref in kv_parts:
        width = ref.shape[0]
        weights = jnp.exp2((scores[:, base : base + width] - row_max) * scale)
        for i in range(width // BLK):
            total += weights[:, i * BLK : (i + 1) * BLK]
        numer += jnp.dot(
            weights.astype(jnp.bfloat16), ref[:, dim:], preferred_element_type=jnp.float32
        )
        base += width
    row_total = jnp.sum(total, axis=1, keepdims=True)
    stat_lane = lax.broadcasted_iota(jnp.int32, (tokens, LANES), 1)
    stats = jnp.zeros((tokens, LANES), jnp.float32)
    half = tokens // 2
    for h in range(heads):
        at = slice(h * tokens, (h + 1) * tokens)
        stats = jnp.where(stat_lane == h, row_max[at], stats)
        stats = jnp.where(stat_lane == heads + h, row_total[at], stats)
        part = numer[at]
        keep[:, h * dim : (h + 1) * dim] = part[:half]
        send[:, h * dim : (h + 1) * dim] = part[half:]
    keep[:, heads * dim :] = stats[:half]
    send[:, heads * dim :] = stats[half:]


def combine(heads, dim, left, right):
    scale = math.log2(math.e) / math.sqrt(dim)
    feature = heads * dim
    stat_left, stat_right = left[:, feature:], right[:, feature:]
    top = jnp.maximum(stat_left, stat_right)
    lane = lax.broadcasted_iota(jnp.int32, top.shape, 1)
    is_max = lane < heads
    shrink_left = jnp.where(is_max, jnp.exp2((stat_left - top) * scale), 0.0)
    shrink_right = jnp.where(is_max, jnp.exp2((stat_right - top) * scale), 0.0)
    moved_left = pltpu.roll(shrink_left, heads, 1)
    moved_right = pltpu.roll(shrink_right, heads, 1)
    stats = jnp.where(is_max, top, stat_left * moved_left + stat_right * moved_right)
    parts = [
        left[:, h * dim : (h + 1) * dim] * shrink_left[:, h : h + 1]
        + right[:, h * dim : (h + 1) * dim] * shrink_right[:, h : h + 1]
        for h in range(heads)
    ]
    return parts, stats


def merge_kernel(heads, dim, left, right, keep, send):
    parts, stats = combine(heads, dim, left, right)
    half = keep.shape[0]
    for h, part in enumerate(parts):
        keep[:, h * dim : (h + 1) * dim] = part[:half]
        send[:, h * dim : (h + 1) * dim] = part[half:]
    keep[:, heads * dim :] = stats[:half]
    send[:, heads * dim :] = stats[half:]


def finish_kernel(heads, dim, left, right, out):
    parts, stats = combine(heads, dim, left, right)
    for h, part in enumerate(parts):
        total = stats[:, heads + h : heads + h + 1]
        out[:, h * dim : (h + 1) * dim] = (part / total).astype(out.dtype)


def in_vmem():
    return pl.BlockSpec(memory_space=pltpu.VMEM)


def per_device(queries, key_value, block_lists):
    columns = lax.axis_size("kcol")
    column = lax.axis_index("kcol")
    row_count = lax.axis_size("qrow")
    row_index = lax.axis_index("qrow")
    tok_dev, feature = queries.shape
    dim = key_value.shape[1] // 2
    heads = feature // dim
    stored = key_value.shape[0] // BLK
    groups = block_lists.shape[0]
    first_query = (stored * columns - groups) * BLK
    masks = [columns >> k for k in range(1, columns.bit_length() - 1)]
    half = stored // 2

    gathered = queries
    for mask in masks:
        arrived = lax.ppermute(gathered, "kcol", swap_pairs(columns, mask))
        if mask != masks[-1]:
            gathered = jnp.concatenate([gathered, arrived], axis=0)
    tokens = 2 * gathered.shape[0]

    mine = lax.dynamic_slice_in_dim(key_value, row_index * half * BLK, half * BLK, 0)
    near = lax.ppermute(mine, "kcol", swap_pairs(columns, 1))
    far = lax.ppermute(near, "qrow", swap_pairs(row_count, 1))

    local = jnp.arange(stored, dtype=jnp.int32)
    other = (column ^ 1) * stored
    ids = jnp.concatenate(
        [
            column * stored + local,
            other + row_index * half + local[:half],
            other + (1 - row_index) * half + local[:half],
        ]
    )
    listed = jnp.any(block_lists[:, :, None] == ids[None, None, :], axis=1).astype(jnp.int32)
    info = jnp.concatenate([listed.reshape(-1), ids, jnp.stack([column, row_index]).astype(jnp.int32)])

    spans = (max(stored - groups, 0), max(half - groups, 0), max(half - groups, 0))
    plan = (tokens, heads, dim, groups, tuple(masks), tok_dev, row_count, first_query, spans)
    width = feature + LANES
    rows = tokens // 2
    message = jax.ShapeDtypeStruct((rows, width), jnp.float32)
    keep, send = pl.pallas_call(
        functools.partial(attend_kernel, plan),
        out_shape=(message, message),
        in_specs=[pl.BlockSpec(memory_space=pltpu.SMEM)] + [in_vmem()] * 5,
        out_specs=(in_vmem(), in_vmem()),
        scratch_shapes=[pltpu.VMEM((heads * tokens, 2 * stored * BLK), jnp.float32)],
        compiler_params=pltpu.CompilerParams(vmem_limit_bytes=32 * 2**20),
        name="attend",
    )(info, gathered, arrived, key_value, near, far)

    for mask in reversed(masks):
        arrived = lax.ppermute(send, "kcol", swap_pairs(columns, mask))
        if mask != masks[0]:
            rows //= 2
            message = jax.ShapeDtypeStruct((rows, width), jnp.float32)
            keep, send = pl.pallas_call(
                functools.partial(merge_kernel, heads, dim),
                out_shape=(message, message),
                in_specs=[in_vmem()] * 2,
                out_specs=(in_vmem(), in_vmem()),
                compiler_params=pltpu.CompilerParams(vmem_limit_bytes=8 * 2**20),
                name="merge",
            )(keep, arrived)
    return pl.pallas_call(
        functools.partial(finish_kernel, heads, dim),
        out_shape=jax.ShapeDtypeStruct((tok_dev, feature), jnp.bfloat16),
        in_specs=[in_vmem()] * 2,
        out_specs=in_vmem(),
        compiler_params=pltpu.CompilerParams(vmem_limit_bytes=8 * 2**20),
        name="finish",
    )(keep, arrived)


def solution(mesh):
    placed = (P(("groups", "kcol", "qrow"), None), P(("groups", "kcol"), None), P("groups", None))
    return jax.shard_map(
        per_device,
        mesh=mesh,
        in_specs=placed,
        out_specs=P(("groups", "kcol", "qrow"), None),
        check_vma=False,
    )
```

time: 170 us -> 37.8 us (0.22)
  blocking collectives: 119 us -> 0 us
  local copies, waits for them, and re-layouts: 19.7 us -> 1.21 us
  waiting for transfers between devices: 0.02 us -> 17.1 us
  starting transfers between devices: 0.01 us -> 15.8 us
  other arithmetic: 14.2 us -> 0.3 us
  between operations: 13.5 us -> 0.05 us
  Pallas kernels: 0 us -> 3.14 us
  matrix products: 3.06 us -> 0 us
    all_gather x3 -> x0, blocking collectives: 119 us -> none  [the longest x2 75.2 us: combined_all(): gathered = jax.tree.map(lambda a: lax.all_gather(a, axis), part)]
    ppermute x0 -> x8, waiting for transfers between devices: none -> 17.1 us  [the longest x3 6.91 us: per_device(): arrived = lax.ppermute(send, 'kcol', swap_pairs(columns, mask))]
    ppermute x0 -> x8, starting transfers between devices: none -> 15.8 us  [the longest x3 6.45 us: per_device(): arrived = lax.ppermute(send, 'kcol', swap_pairs(columns, mask))]
    dynamic_slice x20 -> x1, local copies, waits for them, and re-layouts: 15.7 us -> 1.11 us  [per_device(): lax.dynamic_slice_in_dim(key_value, row_index * half * BLK, half * BLK, 0)]
    add x33 -> x2, other arithmetic: 4.72 us -> 0.01 us  [the longest x1 0.01 us: per_device(): other + row_index * half + local[:half]]
    gather x1 -> x0, other arithmetic: 4.49 us -> none  [one_block(): usable = jnp.repeat(listed_here, BLK, total_repeat_length=stored * BLK)]
    select_n x1 -> x0, other arithmetic: 3.21 us -> none  [one_block(): usable = jnp.repeat(listed_here, BLK, total_repeat_length=stored * BLK)]
    pallas_call x0 -> x4, Pallas kernels: none -> 3.14 us  [the longest x1 2.14 us: per_device(): pl.pallas_call(functools.partial(attend_kernel, plan), out_shape=(message...]
  transfers between devices with their start and end apart: 1 -> 8, of which waited for: 0 -> 6; matrix products, arithmetic and copies ran while one was open for 0% -> 1% of each run, Pallas kernels for 0% -> 0%
where the time goes in v1:
time: 37.8 us; the launch traced here: 37.6 us
  waiting for transfers between devices  17.1 us (45%)
  starting transfers between devices  15.8 us (42%)
  Pallas kernels  3.14 us (8%)
  local copies, waits for them, and re-layouts  1.21 us (3%)
    ppermute x3, waiting for transfers between devices, per_device(): arrived = lax.ppermute(send, 'kcol', swap_pairs(columns, mask))  6.91 us
    ppermute x1, waiting for transfers between devices, per_device(): near = lax.ppermute(mine, 'kcol', swap_pairs(columns, 1))  6.51 us
    ppermute x3, starting transfers between devices, per_device(): arrived = lax.ppermute(send, 'kcol', swap_pairs(columns, mask))  6.45 us
    ppermute x3, starting transfers between devices, per_device(): arrived = lax.ppermute(gathered, 'kcol', swap_pairs(columns, mask))  6.31 us
    ppermute x3, waiting for transfers between devices, per_device(): arrived = lax.ppermute(gathered, 'kcol', swap_pairs(columns, mask))  3.71 us
    ppermute x1, starting transfers between devices, per_device(): near = lax.ppermute(mine, 'kcol', swap_pairs(columns, 1))  3.03 us
    pallas_call x1, Pallas kernels, per_device(): pl.pallas_call(functools.partial(attend_kernel, plan), out_shape=(message...  2.14 us
    dynamic_slice x1, local copies, waits for them, and re-layouts, per_device(): lax.dynamic_slice_in_dim(key_value, row_index * half * BLK, half * BLK, 0)  1.11 us
  transfers between devices with their start and end apart: 8, of which 6 were waited for; matrix products, arithmetic and copies ran while one was open for 1% of the time, Pallas kernels for 0%

profile of v1, /device:TPU:0, one launch (start us, length us, event | category | flops | bytes accessed | tf_op | source)
XLA Modules:
  0.0 37.6 jit_solution(6604226256443155578)
XLA Ops:
  0.0 0.0 copy-start
  0.0 0.0 copy-start.1
  0.0 1.1 %constant_dynamic-slice_fusion = bf16[768,256]{1,0:T(8,128)(2,1)S(1)} fusion(bf16[1536,256]{1,0:T(8,128)(2,1)} %refs_2_.1, s32[]{:T(128)S(6)} %select_n.3), kind=kLoop, calls=%fused_computation.7 | loop fusion | bytes 786436 | tf_op jit(solution)/shard_map/dynamic_slice | solution.py:154
  1.1 3.0 %collective-permute-start.3 = (bf16[768,256]{1,0:T(8,128)(2,1)S(1)}, bf16[768,256]{1,0:T(8,128)(2,1)S(1)}, u32[]{:S(2)}, u32[]{:S(2)}) collective-permute-start(bf16[768,256]{1,0:T(8,128)(2,1)S(1)} %constant_dynamic-slice_fusion), channel_id=1, source_target_pairs={{0,2},{2,0},{4,6},{6,4},{8,10},{10,8},{12,14},{14,12},{16,18},{18,... | collective-permute-start | bytes 1179656 | tf_op jit(solution)/shard_map/ppermute | solution.py:155
  4.1 0.0 copy-done.1
  4.2 2.6 %collective-permute-start = (bf16[4,1024]{1,0:T(4,128)(2,1)S(1)}, bf16[4,1024]{1,0:T(4,128)(2,1)S(1)}, u32[]{:S(2)}, u32[]{:S(2)}) collective-permute-start(bf16[4,1024]{1,0:T(4,128)(2,1)S(1)} %copy-done.1), channel_id=1, source_target_pairs={{0,16},{2,18},{4,20},{6,22},{8,24},{10,26},{12,28},{14,30},{16,0},... | collective-permute-start | bytes 24584 | tf_op jit(solution)/shard_map/ppermute | solution.py:149
  6.8 6.5 %collective-permute-done.3.refs_3_ = bf16[768,256]{1,0:T(8,128)(2,1)S(1)} collective-permute-done((bf16[768,256]{1,0:T(8,128)(2,1)S(1)}, bf16[768,256]{1,0:T(8,128)(2,1)S(1)}, u32[]{:S(2)}, u32[]{:S(2)}) %collective-permute-start.3) | collective-permute-done | bytes 393248 | tf_op jit(solution)/shard_map/ppermute | solution.py:155
  13.3 0.0 collective-permute-start.4
  13.3 0.0 collective-permute-done
  13.3 1.9 %collective-permute-start.1 = (bf16[8,1024]{1,0:T(8,128)(2,1)S(1)}, bf16[8,1024]{1,0:T(8,128)(2,1)S(1)}, u32[]{:S(2)}, u32[]{:S(2)}) collective-permute-start(bf16[8,1024]{1,0:T(8,128)(2,1)S(1)} %pad_maximum_fusion.1), channel_id=1, source_target_pairs={{0,8},{2,10},{4,12},{6,14},{8,0},{10,2},{12,4},{14,6},{16,24},{18,... | collective-permute-start | bytes 49160 | tf_op jit(solution)/shard_map/ppermute | solution.py:149
  15.2 0.1 pad_add_fusion
  15.3 1.8 %collective-permute-done.1 = bf16[8,1024]{1,0:T(8,128)(2,1)S(1)} collective-permute-done((bf16[8,1024]{1,0:T(8,128)(2,1)S(1)}, bf16[8,1024]{1,0:T(8,128)(2,1)S(1)}, u32[]{:S(2)}, u32[]{:S(2)}) %collective-permute-start.1) | collective-permute-done | bytes 16416 | tf_op jit(solution)/shard_map/ppermute | solution.py:149
  17.1 0.0 copy-start.2
  17.1 1.8 %collective-permute-start.2 = (bf16[16,1024]{1,0:T(8,128)(2,1)S(1)}, bf16[16,1024]{1,0:T(8,128)(2,1)S(1)}, u32[]{:S(2)}, u32[]{:S(2)}) collective-permute-start(bf16[16,1024]{1,0:T(8,128)(2,1)S(1)} %pad_maximum_fusion.refs_0_), channel_id=1, source_target_pairs={{0,4},{2,6},{4,0},{6,2},{8,12},{10,14},{12,8},{14,10},{16,20},{18,... | collective-permute-start | bytes 98312 | tf_op jit(solution)/shard_map/ppermute | solution.py:149
  19.0 0.0 copy-done.2
  19.0 0.2 compare_reduce_fusion
  19.2 0.1 concatenate.15.info
  19.2 1.9 %collective-permute-done.2.refs_1_ = bf16[16,1024]{1,0:T(8,128)(2,1)S(1)} collective-permute-done((bf16[16,1024]{1,0:T(8,128)(2,1)S(1)}, bf16[16,1024]{1,0:T(8,128)(2,1)S(1)}, u32[]{:S(2)}, u32[]{:S(2)}) %collective-permute-start.2) | collective-permute-done | bytes 32800 | tf_op jit(solution)/shard_map/ppermute | solution.py:149
  21.1 0.0 collective-permute-done.4.refs_4_
  21.1 0.0 copy-done
  21.1 2.1 %attend.1 = (f32[16,1152]{1,0:T(8,128)S(1)}, f32[16,1152]{1,0:T(8,128)S(1)}) custom-call(s32[50]{0:T(128)S(1)} %concatenate.15.info, bf16[16,1024]{1,0:T(8,128)(2,1)S(1)} %pad_maximum_fusion.refs_0_, bf16[16,1024]{1,0:T(8,128)(2,1)S(1)} %collective-permute-done.2.refs_1_, bf16[1536,256]{1,0:T(8,128)(2,1)S(1)} %copy-done, ...), custom_call_target="tpu_custom_call" | custom-call | tf_op jit(solution)/shard_map/attend/pallas_call | solution.py:175
  23.3 1.8 %collective-permute-start.5 = (f32[16,1152]{1,0:T(8,128)S(1)}, f32[16,1152]{1,0:T(8,128)S(1)}, u32[]{:S(2)}, u32[]{:S(2)}) collective-permute-start(f32[16,1152]{1,0:T(8,128)S(1)} %get-tuple-element.12), channel_id=1, source_target_pairs={{0,4},{2,6},{4,0},{6,2},{8,12},{10,14},{12,8},{14,10},{16,20},{18,... | collective-permute-start | bytes 221192 | tf_op jit(solution)/shard_map/ppermute | solution.py:186
  25.1 2.6 %collective-permute-done.5.right = f32[16,1152]{1,0:T(8,128)S(1)} collective-permute-done((f32[16,1152]{1,0:T(8,128)S(1)}, f32[16,1152]{1,0:T(8,128)S(1)}, u32[]{:S(2)}, u32[]{:S(2)}) %collective-permute-start.5) | collective-permute-done | bytes 73760 | tf_op jit(solution)/shard_map/ppermute | solution.py:186
  27.7 0.1 merge.2
  27.8 1.9 %collective-permute-start.6 = (f32[8,1152]{1,0:T(8,128)S(1)}, f32[8,1152]{1,0:T(8,128)S(1)}, u32[]{:S(2)}, u32[]{:S(2)}) collective-permute-start(f32[8,1152]{1,0:T(8,128)S(1)} %get-tuple-element.14), channel_id=1, source_target_pairs={{0,8},{2,10},{4,12},{6,14},{8,0},{10,2},{12,4},{14,6},{16,24},{18,... | collective-permute-start | bytes 110600 | tf_op jit(solution)/shard_map/ppermute | solution.py:186
  29.7 2.3 %collective-permute-done.6.right = f32[8,1152]{1,0:T(8,128)S(1)} collective-permute-done((f32[8,1152]{1,0:T(8,128)S(1)}, f32[8,1152]{1,0:T(8,128)S(1)}, u32[]{:S(2)}, u32[]{:S(2)}) %collective-permute-start.6) | collective-permute-done | bytes 36896 | tf_op jit(solution)/shard_map/ppermute | solution.py:186
  32.0 0.1 merge.3
  32.1 2.7 %collective-permute-start.7 = (f32[4,1152]{1,0:T(4,128)S(1)}, f32[4,1152]{1,0:T(4,128)S(1)}, u32[]{:S(2)}, u32[]{:S(2)}) collective-permute-start(f32[4,1152]{1,0:T(4,128)S(1)} %get-tuple-element.16), channel_id=1, source_target_pairs={{0,16},{2,18},{4,20},{6,22},{8,24},{10,26},{12,28},{14,30},{16,0},... | collective-permute-start | bytes 55304 | tf_op jit(solution)/shard_map/ppermute | solution.py:186
  34.8 2.0 %collective-permute-done.7.right = f32[4,1152]{1,0:T(4,128)S(1)} collective-permute-done((f32[4,1152]{1,0:T(4,128)S(1)}, f32[4,1152]{1,0:T(4,128)S(1)}, u32[]{:S(2)}, u32[]{:S(2)}) %collective-permute-start.7) | collective-permute-done | bytes 18464 | tf_op jit(solution)/shard_map/ppermute | solution.py:186
  36.9 0.8 %finish.1 = bf16[4,1024]{1,0:T(4,128)(2,1)} custom-call(f32[4,1152]{1,0:T(4,128)S(1)} %get-tuple-element.15.left, f32[4,1152]{1,0:T(4,128)S(1)} %collective-permute-done.7.right), custom_call_target="tpu_custom_call" | custom-call | tf_op jit(solution)/shard_map/finish/pallas_call | solution.py:198
  (6 shorter events, 0.1 us)
Async XLA Ops:
  0.0 21.1 %copy-start = (bf16[1536,256]{1,0:T(8,128)(2,1)S(1)}, bf16[1536,256]{1,0:T(8,128)(2,1)}, u32[]{:S(2)}) copy-start(bf16[1536,256]{1,0:T(8,128)(2,1)} %refs_2_.1) | copy-start | bytes 2359300
  0.0 4.1 %copy-start.1 = (bf16[4,1024]{1,0:T(4,128)(2,1)S(1)}, bf16[4,1024]{1,0:T(4,128)(2,1)}, u32[]{:S(2)}) copy-start(bf16[4,1024]{1,0:T(4,128)(2,1)} %param.3) | copy-start | bytes 24580
  1.1 12.1 %collective-permute-start.3 = (bf16[768,256]{1,0:T(8,128)(2,1)S(1)}, bf16[768,256]{1,0:T(8,128)(2,1)S(1)}, u32[]{:S(2)}, u32[]{:S(2)}) collective-permute-start(bf16[768,256]{1,0:T(8,128)(2,1)S(1)} %constant_dynamic-slice_fusion), channel_id=1, source_target_pairs={{0,2},{2,0},{4,6},{6,4},{8,10},{10,8},{12,14},{14,12},{16,18},{18,... | collective-permute-start | bytes 1179656 | tf_op jit(solution)/shard_map/ppermute | solution.py:155
  4.2 9.1 %collective-permute-start = (bf16[4,1024]{1,0:T(4,128)(2,1)S(1)}, bf16[4,1024]{1,0:T(4,128)(2,1)S(1)}, u32[]{:S(2)}, u32[]{:S(2)}) collective-permute-start(bf16[4,1024]{1,0:T(4,128)(2,1)S(1)} %copy-done.1), channel_id=1, source_target_pairs={{0,16},{2,18},{4,20},{6,22},{8,24},{10,26},{12,28},{14,30},{16,0},... | collective-permute-start | bytes 24584 | tf_op jit(solution)/shard_map/ppermute | solution.py:149
  13.3 7.8 %collective-permute-start.4 = (bf16[768,256]{1,0:T(8,128)(2,1)S(1)}, bf16[768,256]{1,0:T(8,128)(2,1)S(1)}, u32[]{:S(2)}, u32[]{:S(2)}) collective-permute-start(bf16[768,256]{1,0:T(8,128)(2,1)S(1)} %collective-permute-done.3.refs_3_), channel_id=1, source_target_pairs={{0,1},{1,0},{2,3},{3,2},{4,5},{5,4},{6,7},{7,6},{8,9},{9,8},{10,11... | collective-permute-start | bytes 1179656 | tf_op jit(solution)/shard_map/ppermute | solution.py:156
  13.3 3.8 %collective-permute-start.1 = (bf16[8,1024]{1,0:T(8,128)(2,1)S(1)}, bf16[8,1024]{1,0:T(8,128)(2,1)S(1)}, u32[]{:S(2)}, u32[]{:S(2)}) collective-permute-start(bf16[8,1024]{1,0:T(8,128)(2,1)S(1)} %pad_maximum_fusion.1), channel_id=1, source_target_pairs={{0,8},{2,10},{4,12},{6,14},{8,0},{10,2},{12,4},{14,6},{16,24},{18,... | collective-permute-start | bytes 49160 | tf_op jit(solution)/shard_map/ppermute | solution.py:149
  17.1 1.8 %copy-start.2 = (s32[1,64]{1,0:T(1,128)S(1)}, s32[1,64]{1,0:T(1,128)}, u32[]{:S(2)}) copy-start(s32[1,64]{1,0:T(1,128)} %param.5) | copy-start | bytes 772
  17.1 4.0 %collective-permute-start.2 = (bf16[16,1024]{1,0:T(8,128)(2,1)S(1)}, bf16[16,1024]{1,0:T(8,128)(2,1)S(1)}, u32[]{:S(2)}, u32[]{:S(2)}) collective-permute-start(bf16[16,1024]{1,0:T(8,128)(2,1)S(1)} %pad_maximum_fusion.refs_0_), channel_id=1, source_target_pairs={{0,4},{2,6},{4,0},{6,2},{8,12},{10,14},{12,8},{14,10},{16,20},{18,... | collective-permute-start | bytes 98312 | tf_op jit(solution)/shard_map/ppermute | solution.py:149
  23.3 4.4 %collective-permute-start.5 = (f32[16,1152]{1,0:T(8,128)S(1)}, f32[16,1152]{1,0:T(8,128)S(1)}, u32[]{:S(2)}, u32[]{:S(2)}) collective-permute-start(f32[16,1152]{1,0:T(8,128)S(1)} %get-tuple-element.12), channel_id=1, source_target_pairs={{0,4},{2,6},{4,0},{6,2},{8,12},{10,14},{12,8},{14,10},{16,20},{18,... | collective-permute-start | bytes 221192 | tf_op jit(solution)/shard_map/ppermute | solution.py:186
  27.8 4.2 %collective-permute-start.6 = (f32[8,1152]{1,0:T(8,128)S(1)}, f32[8,1152]{1,0:T(8,128)S(1)}, u32[]{:S(2)}, u32[]{:S(2)}) collective-permute-start(f32[8,1152]{1,0:T(8,128)S(1)} %get-tuple-element.14), channel_id=1, source_target_pairs={{0,8},{2,10},{4,12},{6,14},{8,0},{10,2},{12,4},{14,6},{16,24},{18,... | collective-permute-start | bytes 110600 | tf_op jit(solution)/shard_map/ppermute | solution.py:186
  32.1 4.7 %collective-permute-start.7 = (f32[4,1152]{1,0:T(4,128)S(1)}, f32[4,1152]{1,0:T(4,128)S(1)}, u32[]{:S(2)}, u32[]{:S(2)}) collective-permute-start(f32[4,1152]{1,0:T(4,128)S(1)} %get-tuple-element.16), channel_id=1, source_target_pairs={{0,16},{2,18},{4,20},{6,22},{8,24},{10,26},{12,28},{14,30},{16,0},... | collective-permute-start | bytes 55304 | tf_op jit(solution)/shard_map/ppermute | solution.py:186

commit v2 on v1

v2 whole, which is shorter than its diff:
```python
import functools
import math

import jax
import jax.numpy as jnp
from jax import lax
from jax.experimental import pallas as pl
from jax.experimental.pallas import tpu as pltpu
from jax.sharding import PartitionSpec as P


BLK = 128
LANES = 128
AXES = ("kcol", "qrow")
hidden_score = -1e30
floor_score = -1e29


def scale_of(dim):
    return math.log2(math.e) / math.sqrt(dim)


def token_of(plan, info, rows):
    tokens, tok_dev, row_count, masks = plan.tokens, plan.tok_dev, plan.row_count, plan.masks
    column, row_index = info[plan.tail], info[plan.tail + 1]
    t = lax.rem(lax.broadcasted_iota(jnp.int32, (rows, BLK), 0), tokens)
    source = lax.div(t, tok_dev)
    relative = jnp.zeros_like(t)
    crossed = jnp.zeros_like(t)
    for k, mask in enumerate(masks):
        bit = (source >> k) & 1
        relative += bit * mask
        crossed ^= bit
    return ((relative ^ column) * row_count + (crossed ^ row_index)) * tok_dev + lax.rem(t, tok_dev)


def block_scores(plan, info, query, kv, first, scores):
    rows = query.shape[0]
    token = token_of(plan, info, rows)
    lane = lax.broadcasted_iota(jnp.int32, (rows, BLK), 1)
    top = jnp.full((rows, BLK), floor_score, jnp.float32)
    for i in range(plan.stored):
        b = first + i
        bias = jnp.where(info[b] > 0, 0.0, hidden_score).astype(jnp.float32)
        for g in range(1, plan.groups):
            other = jnp.where(info[g * plan.count + b] > 0, 0.0, hidden_score).astype(jnp.float32)
            bias = jnp.where(lax.div(token, BLK) == g, other, bias)
        s = lax.dot_general(
            query,
            kv[i * BLK : (i + 1) * BLK, : plan.dim],
            (((1,), (1,)), ((), ())),
            preferred_element_type=jnp.float32,
        )
        s = s + bias
        if i >= plan.stored - plan.groups:
            key_pos = info[plan.groups * plan.count + b] * BLK + lane
            s = jnp.where(key_pos <= plan.first_query + token, s, hidden_score)
        scores[:, i * BLK : (i + 1) * BLK] = s
        top = jnp.maximum(top, s)
    return jnp.max(top, axis=1, keepdims=True)


def weigh(plan, scores, row_max, values):
    weights = jnp.exp2((scores[...] - row_max) * scale_of(plan.dim))
    total = weights[:, :BLK]
    for i in range(1, plan.stored):
        total = total + weights[:, i * BLK : (i + 1) * BLK]
    numer = jnp.dot(weights.astype(jnp.bfloat16), values, preferred_element_type=jnp.float32)
    return total, numer


def first_kernel(plan, info, first_half, second_half, kv, query_out, numer_out, max_out, total_out, scores):
    dim = plan.dim
    parts = (first_half, second_half)
    query = jnp.concatenate(
        [part[:, h * dim : (h + 1) * dim] for h in range(plan.heads) for part in parts], axis=0
    )
    row_max = block_scores(plan, info, query, kv, 0, scores)
    total, numer = weigh(plan, scores, row_max, kv[:, dim:])
    query_out[...] = query
    numer_out[...] = numer
    max_out[...] = jnp.broadcast_to(row_max, max_out.shape)
    total_out[...] = total


def second_kernel(plan, info, query, numer_in, max_in, total_in, kv, keep, send, scores):
    dim, heads, tokens = plan.dim, plan.heads, plan.tokens
    kv_max = block_scores(plan, info, query[...], kv, plan.stored, scores)
    row_max = jnp.maximum(kv_max, max_in[...])
    shrink = jnp.exp2((max_in[...] - row_max) * scale_of(dim))
    total, numer = weigh(plan, scores, row_max[:, :1], kv[:, dim:])
    numer = numer + numer_in[...] * shrink
    row_total = jnp.sum(total + total_in[...] * shrink, axis=1, keepdims=True)
    stat_lane = lax.broadcasted_iota(jnp.int32, (tokens, LANES), 1)
    stats = jnp.zeros((tokens, LANES), jnp.float32)
    half = tokens // 2
    for h in range(heads):
        at = slice(h * tokens, (h + 1) * tokens)
        stats = jnp.where(stat_lane == h, row_max[at], stats)
        stats = jnp.where(stat_lane == heads + h, row_total[at], stats)
        keep[:, h * dim : (h + 1) * dim] = numer[at][:half]
        send[:, h * dim : (h + 1) * dim] = numer[at][half:]
    keep[:, heads * dim :] = stats[:half]
    send[:, heads * dim :] = stats[half:]


def combine(heads, dim, left, right):
    feature = heads * dim
    stat_left, stat_right = left[:, feature:], right[:, feature:]
    top = jnp.maximum(stat_left, stat_right)
    lane = lax.broadcasted_iota(jnp.int32, top.shape, 1)
    is_max = lane < heads
    shrink_left = jnp.where(is_max, jnp.exp2((stat_left - top) * scale_of(dim)), 0.0)
    shrink_right = jnp.where(is_max, jnp.exp2((stat_right - top) * scale_of(dim)), 0.0)
    moved_left = pltpu.roll(shrink_left, heads, 1)
    moved_right = pltpu.roll(shrink_right, heads, 1)
    stats = jnp.where(is_max, top, stat_left * moved_left + stat_right * moved_right)
    parts = [
        left[:, h * dim : (h + 1) * dim] * shrink_left[:, h : h + 1]
        + right[:, h * dim : (h + 1) * dim] * shrink_right[:, h : h + 1]
        for h in range(heads)
    ]
    return parts, stats


def merge_kernel(heads, dim, left, right, keep, send):
    parts, stats = combine(heads, dim, left, right)
    half = keep.shape[0]
    for h, part in enumerate(parts):
        keep[:, h * dim : (h + 1) * dim] = part[:half]
        send[:, h * dim : (h + 1) * dim] = part[half:]
    keep[:, heads * dim :] = stats[:half]
    send[:, heads * dim :] = stats[half:]


def finish_kernel(heads, dim, left, right, out):
    parts, stats = combine(heads, dim, left, right)
    for h, part in enumerate(parts):
        total = stats[:, heads + h : heads + h + 1]
        out[:, h * dim : (h + 1) * dim] = (part / total).astype(out.dtype)


class Plan:
    def __init__(self, **sizes):
        self.__dict__.update(sizes)


def in_vmem(count):
    return [pl.BlockSpec(memory_space=pltpu.VMEM)] * count


def call(kernel, arguments, outputs, scalars=0, scratch=(), megabytes=8):
    return pl.pallas_call(
        kernel,
        out_shape=outputs,
        in_specs=[pl.BlockSpec(memory_space=pltpu.SMEM)] * scalars
        + in_vmem(len(arguments) - scalars),
        out_specs=tuple(in_vmem(len(outputs))),
        scratch_shapes=scratch,
        compiler_params=pltpu.CompilerParams(vmem_limit_bytes=megabytes * 2**20),
    )(*arguments)


def per_device(queries, key_value, block_lists):
    columns = lax.axis_size("kcol")
    column = lax.axis_index("kcol")
    row_count = lax.axis_size("qrow")
    row_index = lax.axis_index("qrow")
    tok_dev, feature = queries.shape
    dim = key_value.shape[1] // 2
    heads = feature // dim
    stored = key_value.shape[0] // BLK
    groups = block_lists.shape[0]
    masks = [columns >> k for k in range(1, columns.bit_length() - 1)]
    assert columns == 1 << (columns.bit_length() - 1) and row_count == 2

    def across(value, mask):
        pairs = [
            (c * row_count + r, (c ^ mask) * row_count + (r ^ 1))
            for c in range(columns)
            for r in range(row_count)
        ]
        return lax.ppermute(value, AXES, pairs)

    pairs = []
    for c in range(columns):
        pairs += [(c * row_count, (c ^ 1) * row_count + 1), (c * row_count + 1, c * row_count)]
    near = lax.ppermute(key_value, AXES, pairs)
    far = lax.ppermute(near, "qrow", [(0, 1), (1, 0)])

    local = jnp.arange(stored, dtype=jnp.int32)
    ids = jnp.concatenate(
        [(column ^ row_index) * stored + local, (column ^ row_index ^ 1) * stored + local]
    )
    count = 2 * stored
    listed = jnp.any(block_lists[:, :, None] == ids[None, None, :], axis=1).astype(jnp.int32)
    place = jnp.stack([column, row_index]).astype(jnp.int32)
    info = jnp.concatenate([listed.reshape(-1), ids, place])

    staged = lax.optimization_barrier(jnp.pad(queries, ((0, tok_dev), (0, 0))))
    gathered = queries
    for k, mask in enumerate(masks):
        arrived = across(gathered, mask)
        if k == 0 and mask != masks[-1]:
            gathered = staged.at[tok_dev:].set(arrived)
        elif mask != masks[-1]:
            gathered = jnp.concatenate([gathered, arrived], axis=0)
    tokens = 2 * gathered.shape[0]

    plan = Plan(
        tokens=tokens,
        heads=heads,
        dim=dim,
        groups=groups,
        masks=tuple(masks),
        tok_dev=tok_dev,
        row_count=row_count,
        stored=stored,
        count=count,
        tail=(groups + 1) * count,
        first_query=(stored * columns - groups) * BLK,
    )
    rows = heads * tokens

    def f32(*shape):
        return jax.ShapeDtypeStruct(shape, jnp.float32)

    scratch = [pltpu.VMEM((rows, stored * BLK), jnp.float32)]
    begun = call(
        functools.partial(first_kernel, plan),
        (info, gathered, arrived, near),
        (jax.ShapeDtypeStruct((rows, dim), jnp.bfloat16), f32(rows, dim), f32(rows, LANES), f32(rows, LANES)),
        scalars=1,
        scratch=scratch,
        megabytes=24,
    )
    size = tokens // 2
    width = feature + LANES
    keep, send = call(
        functools.partial(second_kernel, plan),
        (info, *begun, far),
        (f32(size, width), f32(size, width)),
        scalars=1,
        scratch=scratch,
        megabytes=24,
    )
    for mask in reversed(masks):
        arrived = across(send, mask)
        if mask != masks[0]:
            size //= 2
            keep, send = call(
                functools.partial(merge_kernel, heads, dim),
                (keep, arrived),
                (f32(size, width), f32(size, width)),
            )
    (out,) = call(
        functools.partial(finish_kernel, heads, dim),
        (keep, arrived),
        (jax.ShapeDtypeStruct((tok_dev, feature), jnp.bfloat16),),
    )
    return out


def solution(mesh):
    placed = (P(("groups", "kcol", "qrow"), None), P(("groups", "kcol"), None), P("groups", None))
    return jax.shard_map(
        per_device,
        mesh=mesh,
        in_specs=placed,
        out_specs=P(("groups", "kcol", "qrow"), None),
        check_vma=False,
    )
```

time: 37.8 us -> 40 us (1.058)
  waiting for transfers between devices: 17.1 us -> 21.7 us
  starting transfers between devices: 15.8 us -> 13 us
  Pallas kernels: 3.14 us -> 3.93 us
    ppermute x8, waiting for transfers between devices: 17.1 us -> 21.7 us  [the longest x6 11.9 us: across(): return lax.ppermute(value, AXES, pairs)]
    ppermute x8, starting transfers between devices: 15.8 us -> 13 us  [the longest x6 9.86 us: across(): return lax.ppermute(value, AXES, pairs)]
    dynamic_slice x1 -> x0, local copies, waits for them, and re-layouts: 1.11 us -> none  [per_device(): lax.dynamic_slice_in_dim(key_value, row_index * half * BLK, half * BLK, 0)]
    pallas_call x4 -> x5, Pallas kernels: 3.14 us -> 3.93 us  [call(): pl.pallas_call(kernel, out_shape=outputs, in_specs=[pl.BlockSpec(memory_s...]
    unnamed x6 -> x4, local copies, waits for them, and re-layouts: 0.01 us -> 0.73 us
  transfers between devices with their start and end apart: 8 -> 8, of which waited for: 6 -> 7; matrix products, arithmetic and copies ran while one was open for 1% -> 1% of each run, Pallas kernels for 0% -> 3%
where the time goes in v2:
time: 40 us; the launch traced here: 39.8 us
  waiting for transfers between devices  21.7 us (54%)
  starting transfers between devices  13 us (32%)
  Pallas kernels  3.93 us (10%)
  local copies, waits for them, and re-layouts  0.83 us (2%)
    ppermute x6, waiting for transfers between devices, across(): return lax.ppermute(value, AXES, pairs)  11.9 us
    ppermute x6, starting transfers between devices, across(): return lax.ppermute(value, AXES, pairs)  9.86 us
    ppermute x1, waiting for transfers between devices, per_device(): near = lax.ppermute(key_value, AXES, pairs)  9.82 us
    pallas_call x5, Pallas kernels, call(): pl.pallas_call(kernel, out_shape=outputs, in_specs=[pl.BlockSpec(memory_s...  3.93 us
    ppermute x1, starting transfers between devices, per_device(): near = lax.ppermute(key_value, AXES, pairs)  2.41 us
  transfers between devices with their start and end apart: 8, of which 7 were waited for; matrix products, arithmetic and copies ran while one was open for 1% of the time, Pallas kernels for 3%

profile of v2, /device:TPU:0, one launch (start us, length us, event | category | flops | bytes accessed | tf_op | source)
XLA Modules:
  0.0 39.8 jit_solution(13730463893517770780)
XLA Ops:
  0.0 2.4 %collective-permute-start.3 = (bf16[1536,256]{1,0:T(8,128)(2,1)}, bf16[1536,256]{1,0:T(8,128)(2,1)S(1)}, u32[]{:S(2)}, u32[]{:S(2)}) collective-permute-start(bf16[1536,256]{1,0:T(8,128)(2,1)} %param.6), channel_id=1, source_target_pairs={{0,3},{1,0},{2,1},{3,2},{4,7},{5,4},{6,5},{7,6},{8,11},{9,8},{10,9... | collective-permute-start | bytes 2359304 | tf_op jit(solution)/shard_map/ppermute | solution.py:188
  2.4 9.8 %collective-permute-done.3.kv = bf16[1536,256]{1,0:T(8,128)(2,1)S(1)} collective-permute-done((bf16[1536,256]{1,0:T(8,128)(2,1)}, bf16[1536,256]{1,0:T(8,128)(2,1)S(1)}, u32[]{:S(2)}, u32[]{:S(2)}) %collective-permute-start.3) | collective-permute-done | bytes 786464 | tf_op jit(solution)/shard_map/ppermute | solution.py:188
  12.2 0.7 %collective-permute-start.4 = (bf16[1536,256]{1,0:T(8,128)(2,1)S(1)}, bf16[1536,256]{1,0:T(8,128)(2,1)S(1)}, u32[]{:S(2)}, u32[]{:S(2)}) collective-permute-start(bf16[1536,256]{1,0:T(8,128)(2,1)S(1)} %collective-permute-done.3.kv), channel_id=1, source_target_pairs={{0,1},{1,0},{2,3},{3,2},{4,5},{5,4},{6,7},{7,6},{8,9},{9,8},{10,11... | collective-permute-start | bytes 2359304 | tf_op jit(solution)/shard_map/ppermute | solution.py:189
  13.0 2.2 %collective-permute-start = (bf16[4,1024]{1,0:T(4,128)(2,1)}, bf16[4,1024]{1,0:T(4,128)(2,1)S(1)}, u32[]{:S(2)}, u32[]{:S(2)}) collective-permute-start(bf16[4,1024]{1,0:T(4,128)(2,1)} %param.5), channel_id=1, source_target_pairs={{0,17},{1,16},{2,19},{3,18},{4,21},{5,20},{6,23},{7,22},{8,25},{9,... | collective-permute-start | bytes 24584 | tf_op jit(solution)/shard_map/ppermute | solution.py:183
  15.2 0.0 copy-start
  15.2 0.7 %copy-done = bf16[4,1024]{1,0:T(4,128)(2,1)S(1)} copy-done((bf16[4,1024]{1,0:T(4,128)(2,1)S(1)}, bf16[4,1024]{1,0:T(4,128)(2,1)}, u32[]{:S(2)}) %copy-start) | copy-done | bytes 8216
  15.9 1.3 %collective-permute-done = bf16[4,1024]{1,0:T(4,128)(2,1)S(1)} collective-permute-done((bf16[4,1024]{1,0:T(4,128)(2,1)}, bf16[4,1024]{1,0:T(4,128)(2,1)S(1)}, u32[]{:S(2)}, u32[]{:S(2)}) %collective-permute-start) | collective-permute-done | bytes 8224 | tf_op jit(solution)/shard_map/ppermute | solution.py:183
  17.2 1.4 %collective-permute-start.1 = (bf16[8,1024]{1,0:T(8,128)(2,1)S(1)}, bf16[8,1024]{1,0:T(8,128)(2,1)S(1)}, u32[]{:S(2)}, u32[]{:S(2)}) collective-permute-start(bf16[8,1024]{1,0:T(8,128)(2,1)S(1)} %constant_dynamic-update-slice_fusion), channel_id=1, source_target_pairs={{0,9},{1,8},{2,11},{3,10},{4,13},{5,12},{6,15},{7,14},{8,1},{9,0},... | collective-permute-start | bytes 49160 | tf_op jit(solution)/shard_map/ppermute | solution.py:183
  18.5 0.1 pad_add_fusion
  18.6 1.8 %collective-permute-done.1 = bf16[8,1024]{1,0:T(8,128)(2,1)S(1)} collective-permute-done((bf16[8,1024]{1,0:T(8,128)(2,1)S(1)}, bf16[8,1024]{1,0:T(8,128)(2,1)S(1)}, u32[]{:S(2)}, u32[]{:S(2)}) %collective-permute-start.1) | collective-permute-done | bytes 16416 | tf_op jit(solution)/shard_map/ppermute | solution.py:183
  20.4 0.0 copy-start.1
  20.4 1.2 %collective-permute-start.2 = (bf16[16,1024]{1,0:T(8,128)(2,1)S(1)}, bf16[16,1024]{1,0:T(8,128)(2,1)S(1)}, u32[]{:S(2)}, u32[]{:S(2)}) collective-permute-start(bf16[16,1024]{1,0:T(8,128)(2,1)S(1)} %pad_maximum_fusion.first_half), channel_id=1, source_target_pairs={{0,5},{1,4},{2,7},{3,6},{4,1},{5,0},{6,3},{7,2},{8,13},{9,12},{10,... | collective-permute-start | bytes 98312 | tf_op jit(solution)/shard_map/ppermute | solution.py:183
  21.6 0.0 copy-done.1
  21.6 0.2 compare_reduce_fusion
  21.8 0.1 concatenate.13.info
  21.9 1.9 %collective-permute-done.2.second_half = bf16[16,1024]{1,0:T(8,128)(2,1)S(1)} collective-permute-done((bf16[16,1024]{1,0:T(8,128)(2,1)S(1)}, bf16[16,1024]{1,0:T(8,128)(2,1)S(1)}, u32[]{:S(2)}, u32[]{:S(2)}) %collective-permute-start.2) | collective-permute-done | bytes 32800 | tf_op jit(solution)/shard_map/ppermute | solution.py:183
  23.8 1.4 %shard_map.40 = (bf16[256,128]{1,0:T(8,128)(2,1)S(1)}, f32[256,128]{1,0:T(8,128)S(1)}, f32[256,128]{1,0:T(8,128)S(1)}, f32[256,128]{1,0:T(8,128)S(1)}) custom-call(s32[50]{0:T(128)S(1)} %concatenate.13.info, bf16[16,1024]{1,0:T(8,128)(2,1)S(1)} %pad_maximum_fusion.first_half, bf16[16,1024]{1,0:T(8,128)(2,1)S(1)} %collective-permute-done.2.second_half, ...), custom_call_target="tpu_custom_call" | custom-call | tf_op jit(solution)/shard_map/pallas_call | solution.py:153
  25.2 0.0 collective-permute-done.4.kv
  25.2 1.6 %shard_map.41 = (f32[16,1152]{1,0:T(8,128)S(1)}, f32[16,1152]{1,0:T(8,128)S(1)}) custom-call(s32[50]{0:T(128)S(1)} %concatenate.13.info, bf16[256,128]{1,0:T(8,128)(2,1)S(1)} %get-tuple-element.27.query, f32[256,128]{1,0:T(8,128)S(1)} %get-tuple-element.28.numer_in, f32[256,128]{1,0:T(8,128)S(1)} %get-tuple-element.29.max_in, ...), custom_call_target="tpu_custom_call" | custom-call | tf_op jit(solution)/shard_map/pallas_call | solution.py:153
  26.8 1.3 %collective-permute-start.5 = (f32[16,1152]{1,0:T(8,128)S(1)}, f32[16,1152]{1,0:T(8,128)S(1)}, u32[]{:S(2)}, u32[]{:S(2)}) collective-permute-start(f32[16,1152]{1,0:T(8,128)S(1)} %get-tuple-element.32), channel_id=1, source_target_pairs={{0,5},{1,4},{2,7},{3,6},{4,1},{5,0},{6,3},{7,2},{8,13},{9,12},{10,... | collective-permute-start | bytes 221192 | tf_op jit(solution)/shard_map/ppermute | solution.py:183
  28.1 3.0 %collective-permute-done.5.right = f32[16,1152]{1,0:T(8,128)S(1)} collective-permute-done((f32[16,1152]{1,0:T(8,128)S(1)}, f32[16,1152]{1,0:T(8,128)S(1)}, u32[]{:S(2)}, u32[]{:S(2)}) %collective-permute-start.5) | collective-permute-done | bytes 73760 | tf_op jit(solution)/shard_map/ppermute | solution.py:183
  31.1 0.1 shard_map.42
  31.2 1.4 %collective-permute-start.6 = (f32[8,1152]{1,0:T(8,128)S(1)}, f32[8,1152]{1,0:T(8,128)S(1)}, u32[]{:S(2)}, u32[]{:S(2)}) collective-permute-start(f32[8,1152]{1,0:T(8,128)S(1)} %get-tuple-element.34), channel_id=1, source_target_pairs={{0,9},{1,8},{2,11},{3,10},{4,13},{5,12},{6,15},{7,14},{8,1},{9,0},... | collective-permute-start | bytes 110600 | tf_op jit(solution)/shard_map/ppermute | solution.py:183
  32.6 2.2 %collective-permute-done.6.right = f32[8,1152]{1,0:T(8,128)S(1)} collective-permute-done((f32[8,1152]{1,0:T(8,128)S(1)}, f32[8,1152]{1,0:T(8,128)S(1)}, u32[]{:S(2)}, u32[]{:S(2)}) %collective-permute-start.6) | collective-permute-done | bytes 36896 | tf_op jit(solution)/shard_map/ppermute | solution.py:183
  34.8 0.1 shard_map.43
  34.9 2.4 %collective-permute-start.7 = (f32[4,1152]{1,0:T(4,128)S(1)}, f32[4,1152]{1,0:T(4,128)S(1)}, u32[]{:S(2)}, u32[]{:S(2)}) collective-permute-start(f32[4,1152]{1,0:T(4,128)S(1)} %get-tuple-element.36), channel_id=1, source_target_pairs={{0,17},{1,16},{2,19},{3,18},{4,21},{5,20},{6,23},{7,22},{8,25},{9,... | collective-permute-start | bytes 55304 | tf_op jit(solution)/shard_map/ppermute | solution.py:183
  37.3 1.8 %collective-permute-done.7.right = f32[4,1152]{1,0:T(4,128)S(1)} collective-permute-done((f32[4,1152]{1,0:T(4,128)S(1)}, f32[4,1152]{1,0:T(4,128)S(1)}, u32[]{:S(2)}, u32[]{:S(2)}) %collective-permute-start.7) | collective-permute-done | bytes 18464 | tf_op jit(solution)/shard_map/ppermute | solution.py:183
  39.0 0.8 %shard_map.44 = bf16[4,1024]{1,0:T(4,128)(2,1)} custom-call(f32[4,1152]{1,0:T(4,128)S(1)} %get-tuple-element.35.left, f32[4,1152]{1,0:T(4,128)S(1)} %collective-permute-done.7.right), custom_call_target="tpu_custom_call" | custom-call | tf_op jit(solution)/shard_map/pallas_call | solution.py:153
  (5 shorter events, 0.0 us)
Async XLA Ops:
  0.0 12.2 %collective-permute-start.3 = (bf16[1536,256]{1,0:T(8,128)(2,1)}, bf16[1536,256]{1,0:T(8,128)(2,1)S(1)}, u32[]{:S(2)}, u32[]{:S(2)}) collective-permute-start(bf16[1536,256]{1,0:T(8,128)(2,1)} %param.6), channel_id=1, source_target_pairs={{0,3},{1,0},{2,1},{3,2},{4,7},{5,4},{6,5},{7,6},{8,11},{9,8},{10,9... | collective-permute-start | bytes 2359304 | tf_op jit(solution)/shard_map/ppermute | solution.py:188
  12.2 12.9 %collective-permute-start.4 = (bf16[1536,256]{1,0:T(8,128)(2,1)S(1)}, bf16[1536,256]{1,0:T(8,128)(2,1)S(1)}, u32[]{:S(2)}, u32[]{:S(2)}) collective-permute-start(bf16[1536,256]{1,0:T(8,128)(2,1)S(1)} %collective-permute-done.3.kv), channel_id=1, source_target_pairs={{0,1},{1,0},{2,3},{3,2},{4,5},{5,4},{6,7},{7,6},{8,9},{9,8},{10,11... | collective-permute-start | bytes 2359304 | tf_op jit(solution)/shard_map/ppermute | solution.py:189
  13.0 4.2 %collective-permute-start = (bf16[4,1024]{1,0:T(4,128)(2,1)}, bf16[4,1024]{1,0:T(4,128)(2,1)S(1)}, u32[]{:S(2)}, u32[]{:S(2)}) collective-permute-start(bf16[4,1024]{1,0:T(4,128)(2,1)} %param.5), channel_id=1, source_target_pairs={{0,17},{1,16},{2,19},{3,18},{4,21},{5,20},{6,23},{7,22},{8,25},{9,... | collective-permute-start | bytes 24584 | tf_op jit(solution)/shard_map/ppermute | solution.py:183
  15.2 0.7 %copy-start = (bf16[4,1024]{1,0:T(4,128)(2,1)S(1)}, bf16[4,1024]{1,0:T(4,128)(2,1)}, u32[]{:S(2)}) copy-start(bf16[4,1024]{1,0:T(4,128)(2,1)} %param.5) | copy-start | bytes 24580
  17.2 3.2 %collective-permute-start.1 = (bf16[8,1024]{1,0:T(8,128)(2,1)S(1)}, bf16[8,1024]{1,0:T(8,128)(2,1)S(1)}, u32[]{:S(2)}, u32[]{:S(2)}) collective-permute-start(bf16[8,1024]{1,0:T(8,128)(2,1)S(1)} %constant_dynamic-update-slice_fusion), channel_id=1, source_target_pairs={{0,9},{1,8},{2,11},{3,10},{4,13},{5,12},{6,15},{7,14},{8,1},{9,0},... | collective-permute-start | bytes 49160 | tf_op jit(solution)/shard_map/ppermute | solution.py:183
  20.4 1.2 %copy-start.1 = (s32[1,64]{1,0:T(1,128)S(1)}, s32[1,64]{1,0:T(1,128)}, u32[]{:S(2)}) copy-start(s32[1,64]{1,0:T(1,128)} %param.7) | copy-start | bytes 772
  20.4 3.4 %collective-permute-start.2 = (bf16[16,1024]{1,0:T(8,128)(2,1)S(1)}, bf16[16,1024]{1,0:T(8,128)(2,1)S(1)}, u32[]{:S(2)}, u32[]{:S(2)}) collective-permute-start(bf16[16,1024]{1,0:T(8,128)(2,1)S(1)} %pad_maximum_fusion.first_half), channel_id=1, source_target_pairs={{0,5},{1,4},{2,7},{3,6},{4,1},{5,0},{6,3},{7,2},{8,13},{9,12},{10,... | collective-permute-start | bytes 98312 | tf_op jit(solution)/shard_map/ppermute | solution.py:183
  26.8 4.3 %collective-permute-start.5 = (f32[16,1152]{1,0:T(8,128)S(1)}, f32[16,1152]{1,0:T(8,128)S(1)}, u32[]{:S(2)}, u32[]{:S(2)}) collective-permute-start(f32[16,1152]{1,0:T(8,128)S(1)} %get-tuple-element.32), channel_id=1, source_target_pairs={{0,5},{1,4},{2,7},{3,6},{4,1},{5,0},{6,3},{7,2},{8,13},{9,12},{10,... | collective-permute-start | bytes 221192 | tf_op jit(solution)/shard_map/ppermute | solution.py:183
  31.2 3.5 %collective-permute-start.6 = (f32[8,1152]{1,0:T(8,128)S(1)}, f32[8,1152]{1,0:T(8,128)S(1)}, u32[]{:S(2)}, u32[]{:S(2)}) collective-permute-start(f32[8,1152]{1,0:T(8,128)S(1)} %get-tuple-element.34), channel_id=1, source_target_pairs={{0,9},{1,8},{2,11},{3,10},{4,13},{5,12},{6,15},{7,14},{8,1},{9,0},... | collective-permute-start | bytes 110600 | tf_op jit(solution)/shard_map/ppermute | solution.py:183
  34.9 4.2 %collective-permute-start.7 = (f32[4,1152]{1,0:T(4,128)S(1)}, f32[4,1152]{1,0:T(4,128)S(1)}, u32[]{:S(2)}, u32[]{:S(2)}) collective-permute-start(f32[4,1152]{1,0:T(4,128)S(1)} %get-tuple-element.36), channel_id=1, source_target_pairs={{0,17},{1,16},{2,19},{3,18},{4,21},{5,20},{6,23},{7,22},{8,25},{9,... | collective-permute-start | bytes 55304 | tf_op jit(solution)/shard_map/ppermute | solution.py:183

commit v3 on v2

v3 whole, which is shorter than its diff:
```python
import functools
import math

import jax
import jax.numpy as jnp
from jax import lax
from jax.experimental import pallas as pl
from jax.experimental.pallas import tpu as pltpu
from jax.sharding import PartitionSpec as P


BLK = 128
LANES = 128
AXES = ("kcol", "qrow")
hidden_score = -(2.0**100)
floor_score = -(2.0**96)


def scale_of(dim):
    return math.log2(math.e) / math.sqrt(dim)


def token_of(plan, rows, offset):
    column, row_index = lax.axis_index("kcol"), lax.axis_index("qrow")
    t = lax.broadcasted_iota(jnp.int32, (plan.half, BLK), 0) + offset
    source = lax.div(t, plan.tok_dev)
    relative = jnp.zeros_like(t)
    crossed = jnp.zeros_like(t)
    for k, mask in enumerate(plan.masks):
        bit = (source >> k) & 1
        relative += bit * mask
        crossed ^= bit
    place = (relative ^ column) * plan.row_count + (crossed ^ row_index)
    token = place * plan.tok_dev + lax.rem(t, plan.tok_dev)
    return jnp.concatenate([token] * (rows // plan.half), axis=0)


def block_scores(plan, bias, query, kv, part, offset, scores):
    rows = query.shape[0]
    token = token_of(plan, rows, offset)
    lane = lax.broadcasted_iota(jnp.int32, (rows, BLK), 1)
    origin = (lax.axis_index("kcol") ^ lax.axis_index("qrow") ^ part) * plan.stored
    top = jnp.full((rows, BLK), floor_score, jnp.float32)
    pack = 2 if plan.stored % 2 == 0 else 1
    for p in range(plan.stored // pack):
        wide = lax.dot_general(
            query,
            kv[p * pack * BLK : (p + 1) * pack * BLK, : plan.dim],
            (((1,), (1,)), ((), ())),
            preferred_element_type=jnp.float32,
        )
        for k in range(pack):
            i = p * pack + k
            b = part * plan.stored + i
            s = wide[:, k * BLK : (k + 1) * BLK]
            offset_row = bias[0, b : b + 1, :]
            for g in range(1, plan.groups):
                offset_row = jnp.where(lax.div(token, BLK) == g, bias[g, b : b + 1, :], offset_row)
            s = s + offset_row
            if i >= plan.stored - plan.groups:
                key_pos = (origin + i) * BLK + lane
                s = jnp.where(key_pos <= plan.first_query + token, s, hidden_score)
            scores[:, b * BLK : (b + 1) * BLK] = s
            top = jnp.maximum(top, s)
    return top


def weigh(plan, scores, first, row_max, values):
    at = slice(first * BLK, (first + plan.stored) * BLK)
    weights = jnp.exp2((scores[:, at] - row_max) * scale_of(plan.dim))
    total = weights[:, :BLK]
    for i in range(1, plan.stored):
        total = total + weights[:, i * BLK : (i + 1) * BLK]
    numer = jnp.dot(weights.astype(jnp.bfloat16), values, preferred_element_type=jnp.float32)
    return total, numer


def stack_heads(plan, tile):
    dim = plan.dim
    return jnp.concatenate([tile[:, h * dim : (h + 1) * dim] for h in range(plan.heads)], axis=0)


def stack_stats(plan, row_max, row_total):
    lane = lax.broadcasted_iota(jnp.int32, (plan.half, LANES), 1)
    stats = jnp.zeros((plan.half, LANES), jnp.float32)
    for h in range(plan.heads):
        at = slice(h * plan.half, (h + 1) * plan.half)
        stats = jnp.where(lane == h, row_max[at], stats)
        stats = jnp.where(lane == plan.heads + h, row_total[at], stats)
    return stats


def put_kept(out, parts, stats):
    dim = parts[0].shape[1]
    for h, part in enumerate(parts):
        out[:, h * dim : (h + 1) * dim] = part
    out[:, len(parts) * dim :] = stats


def put_sent(out, parts, stats):
    dim = parts[0].shape[1]
    for h, part in enumerate(parts):
        out[:, h * dim : (h + 1) * dim] = part.astype(out.dtype)
    high = stats.astype(out.dtype)
    at = len(parts) * dim
    out[:, at : at + LANES] = high
    out[:, at + LANES :] = (stats - high.astype(jnp.float32)).astype(out.dtype)


def shift_of(row_max):
    return row_max.astype(jnp.bfloat16).astype(jnp.float32)


def by_head(plan, stacked):
    return [stacked[h * plan.half : (h + 1) * plan.half] for h in range(plan.heads)]


def first_kernel(plan, bias, tile, kv, numer_out, max_out, total_out, scores):
    query = stack_heads(plan, tile)
    top = block_scores(plan, bias, query, kv, 0, plan.half, scores)
    row_max = jnp.max(top, axis=1, keepdims=True)
    total, numer = weigh(plan, scores, 0, row_max, kv[:, plan.dim :])
    numer_out[...] = numer
    max_out[...] = jnp.broadcast_to(row_max, max_out.shape)
    total_out[...] = total


def second_kernel(plan, bias, tile, numer_in, max_in, total_in, kv, send, scores):
    query = stack_heads(plan, tile)
    top = block_scores(plan, bias, query, kv, 1, plan.half, scores)
    row_max = jnp.maximum(jnp.max(top, axis=1, keepdims=True), max_in[...])
    shrink = jnp.exp2((max_in[...] - row_max) * scale_of(plan.dim))
    total, numer = weigh(plan, scores, plan.stored, row_max[:, :1], kv[:, plan.dim :])
    shift = shift_of(row_max)
    grow = jnp.exp2((row_max - shift) * scale_of(plan.dim))
    numer = (numer + numer_in[...] * shrink) * grow
    row_total = jnp.sum((total + total_in[...] * shrink) * grow, axis=1, keepdims=True)
    put_sent(send, by_head(plan, numer), stack_stats(plan, shift, row_total))


def whole_kernel(plan, bias, tile, near, far, keep, scores):
    query = stack_heads(plan, tile)
    top = jnp.maximum(
        block_scores(plan, bias, query, near, 0, 0, scores),
        block_scores(plan, bias, query, far, 1, 0, scores),
    )
    row_max = jnp.max(top, axis=1, keepdims=True)
    total, numer = weigh(plan, scores, 0, row_max, near[:, plan.dim :])
    more_total, more_numer = weigh(plan, scores, plan.stored, row_max, far[:, plan.dim :])
    row_total = jnp.sum(total + more_total, axis=1, keepdims=True)
    put_kept(keep, by_head(plan, numer + more_numer), stack_stats(plan, row_max, row_total))


def combine(heads, dim, left, right):
    feature = heads * dim
    stat_left = left[:, feature:]
    stat_right = right[:, feature : feature + LANES].astype(jnp.float32)
    stat_right = stat_right + right[:, feature + LANES :].astype(jnp.float32)
    top = shift_of(jnp.maximum(stat_left, stat_right))
    is_max = lax.broadcasted_iota(jnp.int32, top.shape, 1) < heads
    shrink_left = jnp.where(is_max, jnp.exp2((stat_left - top) * scale_of(dim)), 0.0)
    shrink_right = jnp.where(is_max, jnp.exp2((stat_right - top) * scale_of(dim)), 0.0)
    moved_left = pltpu.roll(shrink_left, heads, 1)
    moved_right = pltpu.roll(shrink_right, heads, 1)
    stats = jnp.where(is_max, top, stat_left * moved_left + stat_right * moved_right)
    parts = [
        left[:, h * dim : (h + 1) * dim] * shrink_left[:, h : h + 1]
        + right[:, h * dim : (h + 1) * dim].astype(jnp.float32) * shrink_right[:, h : h + 1]
        for h in range(heads)
    ]
    return parts, stats


def merge_kernel(heads, dim, left, right, keep, send):
    parts, stats = combine(heads, dim, left, right)
    half = keep.shape[0]
    put_kept(keep, [part[:half] for part in parts], stats[:half])
    put_sent(send, [part[half:] for part in parts], stats[half:])


def finish_kernel(heads, dim, left, right, out):
    parts, stats = combine(heads, dim, left, right)
    for h, part in enumerate(parts):
        total = stats[:, heads + h : heads + h + 1]
        out[:, h * dim : (h + 1) * dim] = (part / total).astype(out.dtype)


class Plan:
    def __init__(self, **sizes):
        self.__dict__.update(sizes)


def in_vmem(count):
    return [pl.BlockSpec(memory_space=pltpu.VMEM)] * count


def call(kernel, arguments, outputs, scratch=(), megabytes=8):
    return pl.pallas_call(
        kernel,
        out_shape=outputs,
        in_specs=in_vmem(len(arguments)),
        out_specs=tuple(in_vmem(len(outputs))),
        scratch_shapes=scratch,
        compiler_params=pltpu.CompilerParams(vmem_limit_bytes=megabytes * 2**20),
    )(*arguments)


def per_device(queries, key_value, block_lists):
    columns = lax.axis_size("kcol")
    column = lax.axis_index("kcol")
    row_count = lax.axis_size("qrow")
    row_index = lax.axis_index("qrow")
    tok_dev, feature = queries.shape
    dim = key_value.shape[1] // 2
    heads = feature // dim
    stored = key_value.shape[0] // BLK
    groups = block_lists.shape[0]
    masks = [columns >> k for k in range(1, columns.bit_length() - 1)]
    assert columns == 1 << (columns.bit_length() - 1) and row_count == 2

    def across(value, mask):
        pairs = [
            (c * row_count + r, (c ^ mask) * row_count + (r ^ 1))
            for c in range(columns)
            for r in range(row_count)
        ]
        return lax.ppermute(value, AXES, pairs)

    pairs = []
    for c in range(columns):
        pairs += [(c * row_count, (c ^ 1) * row_count + 1), (c * row_count + 1, c * row_count)]
    near = lax.ppermute(key_value, AXES, pairs)
    far = lax.ppermute(near, "qrow", [(0, 1), (1, 0)])

    local = jnp.arange(stored, dtype=jnp.int32)
    ids = jnp.concatenate(
        [(column ^ row_index) * stored + local, (column ^ row_index ^ 1) * stored + local]
    )
    count = 2 * stored
    listed = jnp.any(block_lists[:, :, None] == ids[None, None, :], axis=1)
    bias = jnp.broadcast_to(
        jnp.where(listed, 0.0, hidden_score)[:, :, None], (groups, count, LANES)
    ).astype(jnp.float32)

    staged = lax.optimization_barrier(jnp.pad(queries, ((0, tok_dev), (0, 0))))
    gathered = queries
    for k, mask in enumerate(masks):
        arrived = across(gathered, mask)
        if k == 0 and mask != masks[-1]:
            gathered = staged.at[tok_dev:].set(arrived)
        elif mask != masks[-1]:
            gathered = jnp.concatenate([gathered, arrived], axis=0)
    tokens = 2 * gathered.shape[0]

    plan = Plan(
        half=tokens // 2,
        heads=heads,
        dim=dim,
        groups=groups,
        masks=tuple(masks),
        tok_dev=tok_dev,
        row_count=row_count,
        stored=stored,
        first_query=(stored * columns - groups) * BLK,
    )
    size = tokens // 2
    rows = heads * size
    width = feature + LANES

    def f32(*shape):
        return jax.ShapeDtypeStruct(shape, jnp.float32)

    def sent(count):
        return jax.ShapeDtypeStruct((count, width + LANES), jnp.bfloat16)

    scratch = [pltpu.VMEM((rows, count * BLK), jnp.float32)]
    begun = call(
        functools.partial(first_kernel, plan),
        (bias, arrived, near),
        (f32(rows, dim), f32(rows, LANES), f32(rows, LANES)),
        scratch=scratch,
        megabytes=24,
    )
    (send,) = call(
        functools.partial(second_kernel, plan),
        (bias, arrived, *begun, far),
        (sent(size),),
        scratch=scratch,
        megabytes=24,
    )
    (keep,) = call(
        functools.partial(whole_kernel, plan),
        (bias, gathered, near, far),
        (f32(size, width),),
            scratch=scratch,
        megabytes=24,
    )
    for mask in reversed(masks):
        arrived = across(send, mask)
        if mask != masks[0]:
            size //= 2
            keep, send = call(
                functools.partial(merge_kernel, heads, dim),
                (keep, arrived),
                (f32(size, width), sent(size)),
            )
    (out,) = call(
        functools.partial(finish_kernel, heads, dim),
        (keep, arrived),
        (jax.ShapeDtypeStruct((tok_dev, feature), jnp.bfloat16),),
    )
    return out


def solution(mesh):
    placed = (P(("groups", "kcol", "qrow"), None), P(("groups", "kcol"), None), P("groups", None))
    return jax.shard_map(
        per_device,
        mesh=mesh,
        in_specs=placed,
        out_specs=P(("groups", "kcol", "qrow"), None),
        check_vma=False,
    )
```

time: 40 us -> 33.3 us (0.83)
  waiting for transfers between devices: 21.7 us -> 16.9 us
  local copies, waits for them, and re-layouts: 0.83 us -> 0.1 us
  Pallas kernels: 3.93 us -> 3.31 us
  starting transfers between devices: 13 us -> 12.4 us
    ppermute x6, waiting for transfers between devices: 11.9 us -> 8.9 us  [across(): return lax.ppermute(value, AXES, pairs)]
    ppermute x1, waiting for transfers between devices: 9.82 us -> 8.05 us  [per_device(): near = lax.ppermute(key_value, AXES, pairs)]
    unnamed x4, local copies, waits for them, and re-layouts: 0.73 us -> 0.01 us
    pallas_call x5 -> x6, Pallas kernels: 3.93 us -> 3.31 us  [call(): pl.pallas_call(kernel, out_shape=outputs, in_specs=in_vmem(len(arguments)...]
    ppermute x6, starting transfers between devices: 9.86 us -> 9.3 us  [across(): return lax.ppermute(value, AXES, pairs)]
  transfers between devices with their start and end apart: 8 -> 8, of which waited for: 7 -> 6; matrix products, arithmetic and copies ran while one was open for 1% -> 1% of each run, Pallas kernels for 3% -> 5%
where the time goes in v3:
time: 33.3 us; the launch traced here: 33.1 us
  waiting for transfers between devices  16.9 us (51%)
  starting transfers between devices  12.4 us (37%)
  Pallas kernels  3.31 us (10%)
    ppermute x6, starting transfers between devices, across(): return lax.ppermute(value, AXES, pairs)  9.3 us
    ppermute x6, waiting for transfers between devices, across(): return lax.ppermute(value, AXES, pairs)  8.9 us
    ppermute x1, waiting for transfers between devices, per_device(): near = lax.ppermute(key_value, AXES, pairs)  8.05 us
    pallas_call x6, Pallas kernels, call(): pl.pallas_call(kernel, out_shape=outputs, in_specs=in_vmem(len(arguments)...  3.31 us
    ppermute x1, starting transfers between devices, per_device(): near = lax.ppermute(key_value, AXES, pairs)  2.41 us
    ppermute x1, starting transfers between devices, per_device(): far = lax.ppermute(near, 'qrow', [(0, 1), (1, 0)])  0.73 us
  transfers between devices with their start and end apart: 8, of which 6 were waited for; matrix products, arithmetic and copies ran while one was open for 1% of the time, Pallas kernels for 5%

profile of v3, /device:TPU:0, one launch (start us, length us, event | category | flops | bytes accessed | tf_op | source)
XLA Modules:
  0.0 33.1 jit_solution(7225378139897136250)
XLA Ops:
  0.0 2.4 %collective-permute-start.2 = (bf16[1536,256]{1,0:T(8,128)(2,1)}, bf16[1536,256]{1,0:T(8,128)(2,1)S(1)}, u32[]{:S(2)}, u32[]{:S(2)}) collective-permute-start(bf16[1536,256]{1,0:T(8,128)(2,1)} %param.6), channel_id=1, source_target_pairs={{0,3},{1,0},{2,1},{3,2},{4,7},{5,4},{6,5},{7,6},{8,11},{9,8},{10,9... | collective-permute-start | bytes 2359304 | tf_op jit(solution)/shard_map/ppermute | solution.py:232
  2.4 1.8 %collective-permute-start = (bf16[4,1024]{1,0:T(4,128)(2,1)}, bf16[4,1024]{1,0:T(4,128)(2,1)S(1)}, u32[]{:S(2)}, u32[]{:S(2)}) collective-permute-start(bf16[4,1024]{1,0:T(4,128)(2,1)} %param.5), channel_id=1, source_target_pairs={{0,17},{1,16},{2,19},{3,18},{4,21},{5,20},{6,23},{7,22},{8,25},{9,... | collective-permute-start | bytes 24584 | tf_op jit(solution)/shard_map/ppermute | solution.py:227
  4.2 0.0 copy-start
  4.2 8.0 %collective-permute-done.2.near.kv = bf16[1536,256]{1,0:T(8,128)(2,1)S(1)} collective-permute-done((bf16[1536,256]{1,0:T(8,128)(2,1)}, bf16[1536,256]{1,0:T(8,128)(2,1)S(1)}, u32[]{:S(2)}, u32[]{:S(2)}) %collective-permute-start.2) | collective-permute-done | bytes 786464 | tf_op jit(solution)/shard_map/ppermute | solution.py:232
  12.2 0.7 %collective-permute-start.3 = (bf16[1536,256]{1,0:T(8,128)(2,1)S(1)}, bf16[1536,256]{1,0:T(8,128)(2,1)S(1)}, u32[]{:S(2)}, u32[]{:S(2)}) collective-permute-start(bf16[1536,256]{1,0:T(8,128)(2,1)S(1)} %collective-permute-done.2.near.kv), channel_id=1, source_target_pairs={{0,1},{1,0},{2,3},{3,2},{4,5},{5,4},{6,7},{7,6},{8,9},{9,8},{10,11... | collective-permute-start | bytes 2359304 | tf_op jit(solution)/shard_map/ppermute | solution.py:233
  13.0 0.1 pad_add_fusion
  13.0 0.0 copy-done
  13.1 0.0 collective-permute-done
  13.1 0.0 copy-start.1
  13.1 1.2 %collective-permute-start.1 = (bf16[8,1024]{1,0:T(8,128)(2,1)S(1)}, bf16[8,1024]{1,0:T(8,128)(2,1)S(1)}, u32[]{:S(2)}, u32[]{:S(2)}) collective-permute-start(bf16[8,1024]{1,0:T(8,128)(2,1)S(1)} %constant_dynamic-update-slice_fusion), channel_id=1, source_target_pairs={{0,9},{1,8},{2,11},{3,10},{4,13},{5,12},{6,15},{7,14},{8,1},{9,0},... | collective-permute-start | bytes 49160 | tf_op jit(solution)/shard_map/ppermute | solution.py:227
  14.4 0.0 copy-done.1
  14.4 0.2 compare_reduce_fusion
  14.5 1.8 %collective-permute-done.1 = bf16[8,1024]{1,0:T(8,128)(2,1)S(1)} collective-permute-done((bf16[8,1024]{1,0:T(8,128)(2,1)S(1)}, bf16[8,1024]{1,0:T(8,128)(2,1)S(1)}, u32[]{:S(2)}, u32[]{:S(2)}) %collective-permute-start.1) | collective-permute-done | bytes 16416 | tf_op jit(solution)/shard_map/ppermute | solution.py:227
  16.3 1.2 %collective-permute-start.4 = (bf16[16,1024]{1,0:T(8,128)(2,1)S(1)}, bf16[16,1024]{1,0:T(8,128)(2,1)S(1)}, u32[]{:S(2)}, u32[]{:S(2)}) collective-permute-start(bf16[16,1024]{1,0:T(8,128)(2,1)S(1)} %pad_maximum_fusion.tile), channel_id=1, source_target_pairs={{0,5},{1,4},{2,7},{3,6},{4,1},{5,0},{6,3},{7,2},{8,13},{9,12},{10,... | collective-permute-start | bytes 98312 | tf_op jit(solution)/shard_map/ppermute | solution.py:227
  17.6 2.1 %collective-permute-done.4.tile = bf16[16,1024]{1,0:T(8,128)(2,1)S(1)} collective-permute-done((bf16[16,1024]{1,0:T(8,128)(2,1)S(1)}, bf16[16,1024]{1,0:T(8,128)(2,1)S(1)}, u32[]{:S(2)}, u32[]{:S(2)}) %collective-permute-start.4) | collective-permute-done | bytes 32800 | tf_op jit(solution)/shard_map/ppermute | solution.py:227
  19.7 0.1 broadcast_in_dim.18.bias
  19.8 0.6 %shard_map.41 = (f32[128,128]{1,0:T(8,128)S(1)}, f32[128,128]{1,0:T(8,128)S(1)}, f32[128,128]{1,0:T(8,128)S(1)}) custom-call(f32[1,24,128]{2,1,0:T(8,128)S(1)} %broadcast_in_dim.18.bias, bf16[16,1024]{1,0:T(8,128)(2,1)S(1)} %collective-permute-done.4.tile, bf16[1536,256]{1,0:T(8,128)(2,1)S(1)} %collective-permute-done.2.near.kv), custom_call_target="tpu_custom_call" | custom-call | tf_op jit(solution)/shard_map/pallas_call | solution.py:198
  20.4 0.0 collective-permute-done.3.far.kv
  20.4 0.7 %shard_map.42 = bf16[16,1280]{1,0:T(8,128)(2,1)S(1)} custom-call(f32[1,24,128]{2,1,0:T(8,128)S(1)} %broadcast_in_dim.18.bias, bf16[16,1024]{1,0:T(8,128)(2,1)S(1)} %collective-permute-done.4.tile, f32[128,128]{1,0:T(8,128)S(1)} %get-tuple-element.24.numer_in, f32[128,128]{1,0:T(8,128)S(1)} %get-tuple-element.25.max_in, ...), custom_call_target="tpu_custom_call" | custom-call | tf_op jit(solution)/shard_map/pallas_call | solution.py:198
  21.1 1.3 %collective-permute-start.5 = (bf16[16,1280]{1,0:T(8,128)(2,1)S(1)}, bf16[16,1280]{1,0:T(8,128)(2,1)S(1)}, u32[]{:S(2)}, u32[]{:S(2)}) collective-permute-start(bf16[16,1280]{1,0:T(8,128)(2,1)S(1)} %shard_map.42), channel_id=1, source_target_pairs={{0,5},{1,4},{2,7},{3,6},{4,1},{5,0},{6,3},{7,2},{8,13},{9,12},{10,... | collective-permute-start | bytes 122888 | tf_op jit(solution)/shard_map/ppermute | solution.py:227
  22.5 1.0 %shard_map.40.left = f32[16,1152]{1,0:T(8,128)S(1)} custom-call(f32[1,24,128]{2,1,0:T(8,128)S(1)} %broadcast_in_dim.18.bias, bf16[16,1024]{1,0:T(8,128)(2,1)S(1)} %pad_maximum_fusion.tile, bf16[1536,256]{1,0:T(8,128)(2,1)S(1)} %collective-permute-done.2.near.kv, bf16[1536,256]{1,0:T(8,128)(2,1)S(1)} %collective-permute-done.3.far.kv), custom_call_target="tpu_custom_call" | custom-call | tf_op jit(solution)/shard_map/pallas_call | solution.py:198
  23.4 1.3 %collective-permute-done.5.right = bf16[16,1280]{1,0:T(8,128)(2,1)S(1)} collective-permute-done((bf16[16,1280]{1,0:T(8,128)(2,1)S(1)}, bf16[16,1280]{1,0:T(8,128)(2,1)S(1)}, u32[]{:S(2)}, u32[]{:S(2)}) %collective-permute-start.5) | collective-permute-done | bytes 40992 | tf_op jit(solution)/shard_map/ppermute | solution.py:227
  24.8 0.1 shard_map.43
  24.9 1.4 %collective-permute-start.6 = (bf16[8,1280]{1,0:T(8,128)(2,1)S(1)}, bf16[8,1280]{1,0:T(8,128)(2,1)S(1)}, u32[]{:S(2)}, u32[]{:S(2)}) collective-permute-start(bf16[8,1280]{1,0:T(8,128)(2,1)S(1)} %get-tuple-element.28), channel_id=1, source_target_pairs={{0,9},{1,8},{2,11},{3,10},{4,13},{5,12},{6,15},{7,14},{8,1},{9,0},... | collective-permute-start | bytes 61448 | tf_op jit(solution)/shard_map/ppermute | solution.py:227
  26.3 1.9 %collective-permute-done.6.right = bf16[8,1280]{1,0:T(8,128)(2,1)S(1)} collective-permute-done((bf16[8,1280]{1,0:T(8,128)(2,1)S(1)}, bf16[8,1280]{1,0:T(8,128)(2,1)S(1)}, u32[]{:S(2)}, u32[]{:S(2)}) %collective-permute-start.6) | collective-permute-done | bytes 20512 | tf_op jit(solution)/shard_map/ppermute | solution.py:227
  28.2 0.1 shard_map.44
  28.3 2.4 %collective-permute-start.7 = (bf16[4,1280]{1,0:T(4,128)(2,1)S(1)}, bf16[4,1280]{1,0:T(4,128)(2,1)S(1)}, u32[]{:S(2)}, u32[]{:S(2)}) collective-permute-start(bf16[4,1280]{1,0:T(4,128)(2,1)S(1)} %get-tuple-element.30), channel_id=1, source_target_pairs={{0,17},{1,16},{2,19},{3,18},{4,21},{5,20},{6,23},{7,22},{8,25},{9,... | collective-permute-start | bytes 30728 | tf_op jit(solution)/shard_map/ppermute | solution.py:227
  30.7 1.7 %collective-permute-done.7.right = bf16[4,1280]{1,0:T(4,128)(2,1)S(1)} collective-permute-done((bf16[4,1280]{1,0:T(4,128)(2,1)S(1)}, bf16[4,1280]{1,0:T(4,128)(2,1)S(1)}, u32[]{:S(2)}, u32[]{:S(2)}) %collective-permute-start.7) | collective-permute-done | bytes 10272 | tf_op jit(solution)/shard_map/ppermute | solution.py:227
  32.4 0.8 %shard_map.45 = bf16[4,1024]{1,0:T(4,128)(2,1)} custom-call(f32[4,1152]{1,0:T(4,128)S(1)} %get-tuple-element.29.left, bf16[4,1280]{1,0:T(4,128)(2,1)S(1)} %collective-permute-done.7.right), custom_call_target="tpu_custom_call" | custom-call | tf_op jit(solution)/shard_map/pallas_call | solution.py:198
  (5 shorter events, 0.0 us)
Async XLA Ops:
  0.0 12.2 %collective-permute-start.2 = (bf16[1536,256]{1,0:T(8,128)(2,1)}, bf16[1536,256]{1,0:T(8,128)(2,1)S(1)}, u32[]{:S(2)}, u32[]{:S(2)}) collective-permute-start(bf16[1536,256]{1,0:T(8,128)(2,1)} %param.6), channel_id=1, source_target_pairs={{0,3},{1,0},{2,1},{3,2},{4,7},{5,4},{6,5},{7,6},{8,11},{9,8},{10,9... | collective-permute-start | bytes 2359304 | tf_op jit(solution)/shard_map/ppermute | solution.py:232
  2.4 10.7 %collective-permute-start = (bf16[4,1024]{1,0:T(4,128)(2,1)}, bf16[4,1024]{1,0:T(4,128)(2,1)S(1)}, u32[]{:S(2)}, u32[]{:S(2)}) collective-permute-start(bf16[4,1024]{1,0:T(4,128)(2,1)} %param.5), channel_id=1, source_target_pairs={{0,17},{1,16},{2,19},{3,18},{4,21},{5,20},{6,23},{7,22},{8,25},{9,... | collective-permute-start | bytes 24584 | tf_op jit(solution)/shard_map/ppermute | solution.py:227
  4.2 8.9 %copy-start = (bf16[4,1024]{1,0:T(4,128)(2,1)S(1)}, bf16[4,1024]{1,0:T(4,128)(2,1)}, u32[]{:S(2)}) copy-start(bf16[4,1024]{1,0:T(4,128)(2,1)} %param.5) | copy-start | bytes 24580
  12.2 8.2 %collective-permute-start.3 = (bf16[1536,256]{1,0:T(8,128)(2,1)S(1)}, bf16[1536,256]{1,0:T(8,128)(2,1)S(1)}, u32[]{:S(2)}, u32[]{:S(2)}) collective-permute-start(bf16[1536,256]{1,0:T(8,128)(2,1)S(1)} %collective-permute-done.2.near.kv), channel_id=1, source_target_pairs={{0,1},{1,0},{2,3},{3,2},{4,5},{5,4},{6,7},{7,6},{8,9},{9,8},{10,11... | collective-permute-start | bytes 2359304 | tf_op jit(solution)/shard_map/ppermute | solution.py:233
  13.1 1.3 %copy-start.1 = (s32[1,64]{1,0:T(1,128)S(1)}, s32[1,64]{1,0:T(1,128)}, u32[]{:S(2)}) copy-start(s32[1,64]{1,0:T(1,128)} %param.7) | copy-start | bytes 772
  13.1 3.2 %collective-permute-start.1 = (bf16[8,1024]{1,0:T(8,128)(2,1)S(1)}, bf16[8,1024]{1,0:T(8,128)(2,1)S(1)}, u32[]{:S(2)}, u32[]{:S(2)}) collective-permute-start(bf16[8,1024]{1,0:T(8,128)(2,1)S(1)} %constant_dynamic-update-slice_fusion), channel_id=1, source_target_pairs={{0,9},{1,8},{2,11},{3,10},{4,13},{5,12},{6,15},{7,14},{8,1},{9,0},... | collective-permute-start | bytes 49160 | tf_op jit(solution)/shard_map/ppermute | solution.py:227
  16.3 3.4 %collective-permute-start.4 = (bf16[16,1024]{1,0:T(8,128)(2,1)S(1)}, bf16[16,1024]{1,0:T(8,128)(2,1)S(1)}, u32[]{:S(2)}, u32[]{:S(2)}) collective-permute-start(bf16[16,1024]{1,0:T(8,128)(2,1)S(1)} %pad_maximum_fusion.tile), channel_id=1, source_target_pairs={{0,5},{1,4},{2,7},{3,6},{4,1},{5,0},{6,3},{7,2},{8,13},{9,12},{10,... | collective-permute-start | bytes 98312 | tf_op jit(solution)/shard_map/ppermute | solution.py:227
  21.1 3.6 %collective-permute-start.5 = (bf16[16,1280]{1,0:T(8,128)(2,1)S(1)}, bf16[16,1280]{1,0:T(8,128)(2,1)S(1)}, u32[]{:S(2)}, u32[]{:S(2)}) collective-permute-start(bf16[16,1280]{1,0:T(8,128)(2,1)S(1)} %shard_map.42), channel_id=1, source_target_pairs={{0,5},{1,4},{2,7},{3,6},{4,1},{5,0},{6,3},{7,2},{8,13},{9,12},{10,... | collective-permute-start | bytes 122888 | tf_op jit(solution)/shard_map/ppermute | solution.py:227
  24.9 3.3 %collective-permute-start.6 = (bf16[8,1280]{1,0:T(8,128)(2,1)S(1)}, bf16[8,1280]{1,0:T(8,128)(2,1)S(1)}, u32[]{:S(2)}, u32[]{:S(2)}) collective-permute-start(bf16[8,1280]{1,0:T(8,128)(2,1)S(1)} %get-tuple-element.28), channel_id=1, source_target_pairs={{0,9},{1,8},{2,11},{3,10},{4,13},{5,12},{6,15},{7,14},{8,1},{9,0},... | collective-permute-start | bytes 61448 | tf_op jit(solution)/shard_map/ppermute | solution.py:227
  28.3 4.1 %collective-permute-start.7 = (bf16[4,1280]{1,0:T(4,128)(2,1)S(1)}, bf16[4,1280]{1,0:T(4,128)(2,1)S(1)}, u32[]{:S(2)}, u32[]{:S(2)}) collective-permute-start(bf16[4,1280]{1,0:T(4,128)(2,1)S(1)} %get-tuple-element.30), channel_id=1, source_target_pairs={{0,17},{1,16},{2,19},{3,18},{4,21},{5,20},{6,23},{7,22},{8,25},{9,... | collective-permute-start | bytes 30728 | tf_op jit(solution)/shard_map/ppermute | solution.py:227
